TPU v7x, 256 devices: a whole 4x4x8 slice. The times are simulated.
256 devices in a mesh: chol: 64 (over x_lo, z, y), walk: 4 (over x_hi, core).
Axes of the slice: x: 4 (x_hi: 2, x_lo: 2; x = x_hi * 2 + x_lo), y: 4, z: 8, core: 2. Of those that a mesh axis runs over, the one named last changes fastest.
Arguments:
- green: bfloat16 [256, 128, 512], P(('chol', 'walk')), may hold values from -2 to 2
- cholesky_rotated_vectors: bfloat16 [256, 128, 512], P('chol'), may hold values from -0.25 to 0.25
- walker_weight: float32 [256], P(('chol', 'walk')), may hold values from 0.04 to 0.16
Outputs:
- green_cot: float32 [256, 128, 512], P(('chol', 'walk'))
- chol_grad: float32 [256, 128, 512], P('chol', None, 'walk')
All inputs are finite; a program needn't handle non-finite values.
Results may differ from a plain program's by a relative error of at most 0.0029.
Values may be sent and summed in bfloat16 or wider, within the bound.
No kernel may reach another device: no remote copies, remote signals or barrier semaphores. Data moves between devices by JAX's collectives and lax.ppermute only.
A program may use at most 64 MiB of HBM per device.

v0:
```python
import jax
import jax.numpy as jnp
from jax import lax
from jax.experimental import pallas as pl
from jax.experimental.pallas import tpu as pltpu
from jax.sharding import Mesh, PartitionSpec as P


F32 = jnp.float32
BF16 = jnp.bfloat16
AXES = ("xl", "z", "y", "xh", "core")
PLANE = ("xl", "y", "xh")
VMEM = pl.BlockSpec(memory_space=pltpu.VMEM)
HBM = pl.BlockSpec(memory_space=pltpu.HBM)
SMEM = pl.BlockSpec(memory_space=pltpu.SMEM)
EXTRA = 16
MINE = ((0, 0), (1, 0), (1, 2), (2, 0), (2, 2), (3, 1), (3, 3), (4, 1))
THEIRS = ((0, 1), (3, 0), (3, 2), (4, 0), (4, 2), (1, 1), (1, 3), (2, 1))
OFFSETS = (0, 1, 2, 3, 4, -1, -2, -3)


def opposed(block, axis, distance):
    if axis == "x":
        n = lax.axis_size("xl") * lax.axis_size("xh")
        flat = [(x % 2) * (n // 2) + x // 2 for x in range(n)]
        names = ("xl", "xh", "core")
    else:
        n = lax.axis_size(axis)
        flat = list(range(n))
        names = (axis, "core")
    route = []
    for i in range(n):
        route.append((2 * flat[i], 2 * flat[(i + distance) % n]))
        route.append((2 * flat[i] + 1, 2 * flat[(i - distance) % n] + 1))
    return lax.ppermute(block, names, route)


def swap(block):
    return lax.ppermute(block, "core", [(0, 1), (1, 0)])


def hold(x):
    return pltpu.with_memory_space_constraint(x, pltpu.HBM)


def call(body, outs, ins, mib, flops=0, moved=2 << 20, scratch=(), out_specs=None):
    return pl.pallas_call(
        body,
        out_shape=outs,
        in_specs=ins,
        out_specs=jax.tree.map(lambda _: VMEM, outs) if out_specs is None else out_specs,
        scratch_shapes=scratch,
        compiler_params=pltpu.CompilerParams(vmem_limit_bytes=mib << 20),
        cost_estimate=pl.CostEstimate(flops=flops, bytes_accessed=moved, transcendentals=0),
    )


def prepare(position, weight, green, vectors, payload, ordered, sems):
    core = position[0]
    o, m = green.shape[1:]
    copies = [pltpu.make_async_copy(green, payload.at[:, pl.ds(0, o)], sems.at[4])]
    for k, v in enumerate((core, core + 2, 1 - core, 3 - core)):
        copies.append(pltpu.make_async_copy(vectors.at[v], ordered.at[k], sems.at[k]))
    for copy in copies:
        copy.start()
    w = jnp.full((EXTRA, m), weight[0], F32)
    high = w.astype(BF16).astype(F32)
    middle = (w - high).astype(BF16).astype(F32)
    low = w - high - middle
    row = lax.broadcasted_iota(jnp.int32, w.shape, 0)
    tile = jnp.where(row == 0, high, jnp.where(row == 1, middle, jnp.where(row == 2, low, 0.0)))
    payload[0, o:, :] = tile.astype(BF16)
    for copy in copies:
        copy.wait()


def collect(groups, vectors):
    o, _ = groups[0].shape[1:]
    for g, group in enumerate(groups):
        for j in range(2):
            vectors[(2 * g + j) * o : (2 * g + j + 1) * o, :] = group[j]


def multiply(vectors, walkers, exch, scaled=None):
    o = walkers[0].shape[1] - EXTRA
    count = vectors.shape[0] // o
    quad = 4
    places = MINE + THEIRS
    for i in range(len(places) // 2):
        pair = places[2 * i : 2 * i + 2]
        blocks = [walkers[a][k, :o, :] for a, k in pair]
        both = jnp.concatenate(blocks)
        for q in range(count // quad):
            part = lax.dot_general(
                vectors[q * quad * o : (q + 1) * quad * o, :],
                both,
                (((1,), (1,)), ((), ())),
                preferred_element_type=F32,
            ).astype(BF16)
            for g in range(quad):
                for w in range(2):
                    exch[
                        (2 * i + w) * o : (2 * i + w + 1) * o, (q * quad + g) * o : (q * quad + g + 1) * o
                    ] = part[g * o : (g + 1) * o, w * o : (w + 1) * o]
        if scaled is not None:
            for w, (a, k) in enumerate(pair):
                weight = jnp.sum(walkers[a][k, o:, :].astype(F32), axis=0, keepdims=True)
                scaled[i, :, w * o : (w + 1) * o] = (blocks[w].astype(F32) * weight).astype(BF16).T


def reduce_walkers(scaled, exch, store):
    pairs, m, two = scaled.shape
    width = 2 * two
    for c in range(exch.shape[1] // width):
        acc = jnp.zeros((m, width), F32)
        for i in range(pairs):
            acc += jnp.dot(
                scaled[i], exch[i * two : (i + 1) * two, c * width : (c + 1) * width], preferred_element_type=F32
            )
        acc = acc.astype(BF16)
        for s in range(width // two):
            for h in range(2):
                store(c * (width // two) + s, h, acc[h * m // 2 : (h + 1) * m // 2, s * two : (s + 1) * two])


def first(chip, near, rest, w1, w2, v0, v1, v2, v3, exch, scaled, vectors, grad):
    collect((v0, v1, v2, v3), vectors)
    multiply(vectors, (chip, near, rest, w1, w2), exch, scaled)

    def store(group, h, block):
        grad[2 * group + h] = block

    reduce_walkers(scaled, exch, store)


def second(chip, near, rest, w1, w2, v0, v1, v2, v3, exch0, vectors0, exch, cot_mine, cot_theirs, vectors, cot, sems):
    collect((v0, v1, v2, v3), vectors)
    multiply(vectors, (chip, near, rest, w1, w2), exch)
    half = cot_mine.shape[0]
    run = 512
    stores = []
    for r in range(2 * half // run):
        base = (half + r * run) % (2 * half)
        rows = slice(base, base + run)
        part = jnp.dot(exch0[rows, :], vectors0[...], preferred_element_type=F32)
        part += jnp.dot(exch[rows, :], vectors[...], preferred_element_type=F32)
        if base >= half:
            target = slice(base - half, base - half + run)
            cot[target, :] = part.astype(BF16)
            stores.append(pltpu.make_async_copy(cot.at[target], cot_theirs.at[target], sems.at[r]))
            stores[-1].start()
        else:
            cot_mine[rows, :] = part
    for copy in stores:
        copy.wait()


def gradient(position, scaled, exch, grad0, grad, staged, sems):
    core, column, y, rows = position[0], position[1], position[2], position[3]
    step = 2 * core - 1
    places = [lax.rem(y + d + rows, rows) for d in (0, step, 2, -step)]
    copies = []
    for g, place in enumerate(places):
        target = grad.at[pl.ds((column * rows + place) * 2, 2)]
        copies.append(pltpu.make_async_copy(grad0.at[pl.ds(2 * g, 2)], target, sems.at[g]))
        copies[-1].start()

    def store(group, h, block):
        staged[2 * group + h] = block
        if h == 1:
            target = grad.at[pl.ds(((1 - column) * rows + places[group]) * 2, 2)]
            copies.append(pltpu.make_async_copy(staged.at[pl.ds(2 * group, 2)], target, sems.at[4 + group]))
            copies[-1].start()

    reduce_walkers(scaled, exch, store)
    for copy in copies:
        copy.wait()


def join(cot_mine, returned, *refs):
    outs, (staged, sems) = refs[:-2], refs[-2:]
    o = outs[0].shape[0]
    stores = []
    for k, out in enumerate(outs):
        rows = slice(k * o, (k + 1) * o)
        staged[k] = (cot_mine[rows, :] + returned[rows, :].astype(F32)).astype(BF16)
        stores.append(pltpu.make_async_copy(staged.at[k], out, sems.at[k]))
        stores[-1].start()
    for copy in stores:
        copy.wait()


def total(position, parts, keep, send):
    core = position[0]
    rows = keep.shape[0]
    for out, c in ((send, 1 - core), (keep, core)):
        start = pl.multiple_of(c * rows, rows)
        acc = parts[0, pl.ds(start, rows), :].astype(F32)
        for s in range(1, parts.shape[0]):
            acc += parts[s, pl.ds(start, rows), :].astype(F32)
        out[...] = -acc


def place(position, keep, received, out):
    core = position[0]
    n = out.shape[1]
    for h in range(2):
        out[2 * h + core] = keep[:, h * n : (h + 1) * n].T
        out[2 * h + 1 - core] = received[:, h * n : (h + 1) * n].T


def step(green, vectors, weight):
    zs, ys = lax.axis_size("z"), lax.axis_size("y")
    plane = lax.axis_size("xl") * ys * lax.axis_size("xh")
    _, o, m = green.shape
    index = [lax.axis_index(a) for a in ("core", "xl", "y")]
    position = jnp.stack([*index, jnp.int32(ys)]).astype(jnp.int32)
    shape = jax.ShapeDtypeStruct
    dma = pltpu.SemaphoreType.DMA

    payload, ordered = call(
        prepare,
        (pltpu.VMEM((1, o + EXTRA, m), BF16), pltpu.VMEM((4, o, m), BF16)),
        [SMEM, SMEM, HBM, HBM],
        8,
        scratch=[dma((5,))],
    )(position, weight, hold(green), hold(vectors))

    y1 = opposed(ordered, "y", 1)
    chip = jnp.concatenate([payload, swap(payload)])
    z2 = opposed(chip, "z", 2)
    z1 = opposed(chip, "z", 1)
    x0 = opposed(ordered[:2], "x", 1)
    y2 = opposed(y1[:2], "y", 1)
    x1 = opposed(y1, "x", 1)
    y3 = swap(y1[2:])
    z3 = opposed(z2, "z", 1)
    z4 = opposed(z2[:1], "z", 2)
    near = jnp.concatenate([z1, z2])
    w1 = swap(near)
    x2 = opposed(y2, "x", 1)
    x3 = swap(x1[2:])
    rest = jnp.concatenate([z3, z4])
    w2 = swap(rest)

    half = plane // 2
    pair_flops = 2 * o * o * m
    exch0, scaled, vectors0, grad0 = call(
        first,
        (
            pltpu.VMEM((2 * zs * o, half * o), BF16),
            pltpu.VMEM((zs, m, 2 * o), BF16),
            pltpu.VMEM((half * o, m), BF16),
            pltpu.VMEM((half, m // 2, 2 * o), BF16),
        ),
        [VMEM] * 9,
        24,
        flops=2 * zs * plane * pair_flops,
    )(chip, near, rest, w1, w2, ordered, y1, y2, y3)

    exch1, cot_mine, cot_theirs = call(
        second,
        (pltpu.VMEM((2 * zs * o, half * o), BF16), pltpu.VMEM((zs * o, m), F32), pltpu.HBM((zs * o, m), BF16)),
        [VMEM] * 11,
        32,
        flops=3 * zs * plane * pair_flops,
        scratch=[pltpu.VMEM((half * o, m), BF16), pltpu.VMEM((zs * o, m), BF16), dma((4,))],
        out_specs=(VMEM, VMEM, HBM),
    )(chip, near, rest, w1, w2, x0, x1, x2, x3, exch0, vectors0)
    returned = swap(cot_theirs)

    grad = call(
        gradient,
        pltpu.HBM((plane, m // 2, 2 * o), BF16),
        [SMEM, VMEM, VMEM, VMEM],
        24,
        flops=zs * plane * pair_flops,
        scratch=[pltpu.VMEM((half, m // 2, 2 * o), BF16), dma((8,))],
        out_specs=HBM,
    )(position, scaled, exch1, grad0)

    sums = call(
        join,
        tuple(pltpu.HBM((o, m), BF16) for _ in range(zs)),
        [VMEM] * 2,
        16,
        scratch=[pltpu.VMEM((zs, o, m), BF16), dma((zs,))],
        out_specs=(HBM,) * zs,
    )(cot_mine, returned)
    grad, *sums = lax.optimization_barrier((grad, *sums))
    grad = lax.all_to_all(grad, PLANE, 0, 0, tiled=True)
    cot = None
    for k, block in sorted(zip(OFFSETS, sums), key=lambda kb: -abs(kb[0])):
        part = (block if k == 0 else opposed(block, "z", -k)).astype(F32)
        cot = part if cot is None else cot + part
    green_cot = (-weight[0] * cot)[None]

    keep, send = call(total, (shape((m // 4, 2 * o), F32),) * 2, [SMEM, VMEM], 16)(position, grad)
    chol_grad = call(place, shape((4, o, m // 4), F32), [SMEM, VMEM, VMEM], 16)(position, keep, swap(send))
    return green_cot, chol_grad


def solution(mesh):
    grid = Mesh(mesh.devices.reshape(2, 8, 4, 2, 2), AXES)
    chol, walk = ("xl", "z", "y"), ("xh", "core")
    every = chol + walk
    return jax.shard_map(
        step,
        mesh=grid,
        in_specs=(P(every, None, None), P(chol, None, None), P(every)),
        out_specs=(P(every, None, None), P(chol, None, walk)),
        check_vma=False,
    )
```

profile of v0, /device:TPU:1, one launch (start us, length us, event | category | flops | bytes accessed | tf_op | source)
XLA Modules:
  0.0 103.4 jit_solution(8617857221370707388)
XLA Ops:
  1.3 0.1 pad_add_fusion.position
  1.4 1.7 %shard_map.50 = (bf16[1,144,512]{2,1,0:T(8,128)(2,1)S(1)}, bf16[4,128,512]{2,1,0:T(8,128)(2,1)S(1)}) custom-call(s32[4]{0:T(128)S(1)} %pad_add_fusion.position, f32[1]{0:T(128)S(6)} %copy.8.weight, bf16[1,128,512]{2,1,0:T(8,128)(2,1)} %green.1, bf16[4,128,512]{2,1,0:T(8,128)(2,1)} %vectors.1), custom_call_target="tpu_custom_call" | custom-call | bytes 2097152 | tf_op jit(solution)/shard_map/pallas_call | solution.py:221
  3.1 3.3 %collective-permute-start = (bf16[1,144,512]{2,1,0:T(8,128)(2,1)S(1)}, bf16[1,144,512]{2,1,0:T(8,128)(2,1)S(1)}, u32[]{:S(2)}, u32[]{:S(2)}) collective-permute-start(bf16[1,144,512]{2,1,0:T(8,128)(2,1)S(1)} %get-tuple-element.30), channel_id=1, source_target_pairs={{0,1},{1,0},{2,3},{3,2},{4,5},{5,4},{6,7},{7,6},{8,9},{9,8},{10,11... | collective-permute-start | bytes 442376 | tf_op jit(solution)/shard_map/ppermute | solution.py:39
  6.4 1.0 collective-permute-done
  7.4 4.4 %collective-permute-start.2 = (bf16[2,144,512]{2,1,0:T(8,128)(2,1)S(1)}, bf16[2,144,512]{2,1,0:T(8,128)(2,1)S(1)}, u32[]{:S(2)}, u32[]{:S(2)}) collective-permute-start(bf16[2,144,512]{2,1,0:T(8,128)(2,1)S(1)} %constant_dynamic-update-slice_fusion.chip), channel_id=1, source_target_pairs={{0,32},{1,97},{16,48},{17,113},{32,64},{33,1},{48,80},{49,17},{64,... | collective-permute-start | bytes 884744 | tf_op jit(solution)/shard_map/ppermute | solution.py:35
  11.8 0.7 collective-permute-start.1
  12.5 2.7 %collective-permute-start.7 = (bf16[4,128,512]{2,1,0:T(8,128)(2,1)S(1)}, bf16[4,128,512]{2,1,0:T(8,128)(2,1)S(1)}, u32[]{:S(2)}, u32[]{:S(2)}) collective-permute-start(bf16[4,128,512]{2,1,0:T(8,128)(2,1)S(1)} %get-tuple-element.31.v0), channel_id=1, source_target_pairs={{0,4},{1,13},{4,8},{5,1},{8,12},{9,5},{12,0},{13,9},{2,6},{3,15},{... | collective-permute-start | bytes 1572872 | tf_op jit(solution)/shard_map/ppermute | solution.py:35
  15.3 2.2 %collective-permute-done.2 = bf16[2,144,512]{2,1,0:T(8,128)(2,1)S(1)} collective-permute-done((bf16[2,144,512]{2,1,0:T(8,128)(2,1)S(1)}, bf16[2,144,512]{2,1,0:T(8,128)(2,1)S(1)}, u32[]{:S(2)}, u32[]{:S(2)}) %collective-permute-start.2) | collective-permute-done | bytes 294944 | tf_op jit(solution)/shard_map/ppermute | solution.py:35
  17.4 4.5 %collective-permute-start.3 = (bf16[2,144,512]{2,1,0:T(8,128)(2,1)S(1)}, bf16[2,144,512]{2,1,0:T(8,128)(2,1)S(1)}, u32[]{:S(2)}, u32[]{:S(2)}) collective-permute-start(bf16[2,144,512]{2,1,0:T(8,128)(2,1)S(1)} %collective-permute-done.2), channel_id=1, source_target_pairs={{0,16},{1,113},{16,32},{17,1},{32,48},{33,17},{48,64},{49,33},{64,... | collective-permute-start | bytes 884744 | tf_op jit(solution)/shard_map/ppermute | solution.py:35
  21.9 0.7 collective-permute-start.4
  22.6 0.0 collective-permute-done.1
  22.7 0.5 collective-permute-start.5
  23.2 0.0 collective-permute-done.7.v1
  23.2 2.5 %collective-permute-start.11 = (bf16[4,128,512]{2,1,0:T(8,128)(2,1)S(1)}, bf16[4,128,512]{2,1,0:T(8,128)(2,1)S(1)}, u32[]{:S(2)}, u32[]{:S(2)}) collective-permute-start(bf16[4,128,512]{2,1,0:T(8,128)(2,1)S(1)} %collective-permute-done.7.v1), channel_id=1, source_target_pairs={{0,128},{1,131},{128,2},{129,1},{2,130},{3,129},{130,0},{131,3},{4... | collective-permute-start | bytes 1572872 | tf_op jit(solution)/shard_map/ppermute | solution.py:35
  25.7 0.8 collective-permute-done.3
  26.4 2.4 %collective-permute-done.4 = bf16[1,144,512]{2,1,0:T(8,128)(2,1)S(1)} collective-permute-done((bf16[1,144,512]{2,1,0:T(8,128)(2,1)S(1)}, bf16[1,144,512]{2,1,0:T(8,128)(2,1)S(1)}, u32[]{:S(2)}, u32[]{:S(2)}) %collective-permute-start.4) | collective-permute-done | bytes 147488 | tf_op jit(solution)/shard_map/ppermute | solution.py:35
  28.8 2.1 %collective-permute-start.6 = (bf16[3,144,512]{2,1,0:T(8,128)(2,1)S(1)}, bf16[3,144,512]{2,1,0:T(8,128)(2,1)S(1)}, u32[]{:S(2)}, u32[]{:S(2)}) collective-permute-start(bf16[3,144,512]{2,1,0:T(8,128)(2,1)S(1)} %constant_dynamic-update-slice_fusion.4.rest), channel_id=1, source_target_pairs={{0,1},{1,0},{2,3},{3,2},{4,5},{5,4},{6,7},{7,6},{8,9},{9,8},{10,11... | collective-permute-start | bytes 1327112 | tf_op jit(solution)/shard_map/ppermute | solution.py:39
  31.0 2.8 %collective-permute-start.8 = (bf16[2,128,512]{2,1,0:T(8,128)(2,1)S(1)}, bf16[2,128,512]{2,1,0:T(8,128)(2,1)S(1)}, u32[]{:S(2)}, u32[]{:S(2)}) collective-permute-start(bf16[2,128,512]{2,1,0:T(8,128)(2,1)S(1)} %get-tuple-element.59), channel_id=1, source_target_pairs={{0,4},{1,13},{4,8},{5,1},{8,12},{9,5},{12,0},{13,9},{2,6},{3,15},{... | collective-permute-start | bytes 786440 | tf_op jit(solution)/shard_map/ppermute | solution.py:35
  33.8 0.0 collective-permute-start.9
  33.8 3.3 %collective-permute-done.8.v2 = bf16[2,128,512]{2,1,0:T(8,128)(2,1)S(1)} collective-permute-done((bf16[2,128,512]{2,1,0:T(8,128)(2,1)S(1)}, bf16[2,128,512]{2,1,0:T(8,128)(2,1)S(1)}, u32[]{:S(2)}, u32[]{:S(2)}) %collective-permute-start.8) | collective-permute-done | bytes 262176 | tf_op jit(solution)/shard_map/ppermute | solution.py:35
  37.1 2.5 %collective-permute-start.10 = (bf16[2,128,512]{2,1,0:T(8,128)(2,1)S(1)}, bf16[2,128,512]{2,1,0:T(8,128)(2,1)S(1)}, u32[]{:S(2)}, u32[]{:S(2)}) collective-permute-start(bf16[2,128,512]{2,1,0:T(8,128)(2,1)S(1)} %slice.18), channel_id=1, source_target_pairs={{0,128},{1,131},{128,2},{129,1},{2,130},{3,129},{130,0},{131,3},{4... | collective-permute-start | bytes 786440 | tf_op jit(solution)/shard_map/ppermute | solution.py:35
  39.6 0.0 collective-permute-done.11.v1
  39.6 0.5 collective-permute-start.12
  40.1 0.0 collective-permute-done.9.v3
  40.2 1.8 %collective-permute-start.13 = (bf16[2,128,512]{2,1,0:T(8,128)(2,1)S(1)}, bf16[2,128,512]{2,1,0:T(8,128)(2,1)S(1)}, u32[]{:S(2)}, u32[]{:S(2)}) collective-permute-start(bf16[2,128,512]{2,1,0:T(8,128)(2,1)S(1)} %slice.23), channel_id=1, source_target_pairs={{0,1},{1,0},{2,3},{3,2},{4,5},{5,4},{6,7},{7,6},{8,9},{9,8},{10,11... | collective-permute-start | bytes 786440 | tf_op jit(solution)/shard_map/ppermute | solution.py:39
  41.9 0.0 collective-permute-done.5.w1
  41.9 0.0 collective-permute-done.6.w2
  41.9 4.6 %shard_map.51 = (bf16[2048,1024]{1,0:T(8,128)(2,1)S(1)}, bf16[8,512,256]{2,1,0:T(8,128)(2,1)S(1)}, bf16[1024,512]{1,0:T(8,128)(2,1)S(1)}, bf16[8,256,256]{2,1,0:T(8,128)(2,1)S(1)}) custom-call(bf16[2,144,512]{2,1,0:T(8,128)(2,1)S(1)} %constant_dynamic-update-slice_fusion.chip, bf16[4,144,512]{2,1,0:T(8,128)(2,1)S(1)} %constant_dynamic-update-slice_fusion.2.near, ...), custom_call_target="tpu_custom_call" | custom-call | flops 4294967296 | bytes 2097152 | tf_op jit(solution)/shard_map/pallas_call | solution.py:248
  46.5 0.0 collective-permute-done.10.v0
  46.5 0.0 collective-permute-done.12.v2
  46.5 0.0 collective-permute-done.13.v3
  46.5 6.7 %shard_map.52 = (bf16[2048,1024]{1,0:T(8,128)(2,1)S(1)}, f32[1024,512]{1,0:T(8,128)S(1)}, bf16[1024,512]{1,0:T(8,128)(2,1)}) custom-call(bf16[2,144,512]{2,1,0:T(8,128)(2,1)S(1)} %constant_dynamic-update-slice_fusion.chip, bf16[4,144,512]{2,1,0:T(8,128)(2,1)S(1)} %constant_dynamic-update-slice_fusion.2.near, ...), custom_call_target="tpu_custom_call" | custom-call | flops 6442450944 | bytes 2097152 | tf_op jit(solution)/shard_map/pallas_call | solution.py:261
  53.3 2.6 %collective-permute-start.14 = (bf16[1024,512]{1,0:T(8,128)(2,1)}, bf16[1024,512]{1,0:T(8,128)(2,1)S(1)}, u32[]{:S(2)}, u32[]{:S(2)}) collective-permute-start(bf16[1024,512]{1,0:T(8,128)(2,1)} %get-tuple-element.38), channel_id=1, source_target_pairs={{0,1},{1,0},{2,3},{3,2},{4,5},{5,4},{6,7},{7,6},{8,9},{9,8},{10,11... | collective-permute-start | bytes 3145736 | tf_op jit(solution)/shard_map/ppermute | solution.py:39
  55.9 3.8 %shard_map.53 = bf16[16,256,256]{2,1,0:T(8,128)(2,1)} custom-call(s32[4]{0:T(128)S(1)} %pad_add_fusion.position, bf16[8,512,256]{2,1,0:T(8,128)(2,1)S(1)} %get-tuple-element.32.scaled, bf16[2048,1024]{1,0:T(8,128)(2,1)S(1)} %get-tuple-element.35.exch, bf16[8,256,256]{2,1,0:T(8,128)(2,1)S(1)} %get-tuple-element.36.grad0), custom_call_target="tpu_custom_call" | custom-call | flops 2147483648 | bytes 2097152 | tf_op jit(solution)/shard_map/pallas_call | solution.py:272
  59.6 0.0 collective-permute-done.14.returned
  59.7 1.0 %shard_map.54 = (bf16[128,512]{1,0:T(8,128)(2,1)}, bf16[128,512]{1,0:T(8,128)(2,1)}, bf16[128,512]{1,0:T(8,128)(2,1)}, bf16[128,512]{1,0:T(8,128)(2,1)}, bf16[12...) custom-call(f32[1024,512]{1,0:T(8,128)S(1)} %get-tuple-element.37.cot_mine, ...), custom_call_target="tpu_custom_call" | custom-call | bytes 2097152 | tf_op jit(solution)/shard_map/pallas_call | solution.py:282
  60.7 0.0 copy-start.5
  60.7 0.0 copy-start.4
  60.7 0.0 copy-start.2
  60.8 0.0 copy-start.1
  60.8 4.5 %all-to-all-start = ((bf16[16,256,256]{2,1,0:T(8,128)(2,1)}), bf16[16,256,256]{2,1,0:T(8,128)(2,1)S(1)}, u32[]{:S(2)}, u32[]{:S(2)}) async-start(bf16[16,256,256]{2,1,0:T(8,128)(2,1)} %shard_map.53), calls=%async_computation | async-start | bytes 4194304 | tf_op jit(solution)/shard_map/all_to_all | solution.py:291
  65.2 0.0 copy-start
  65.3 3.9 %collective-permute-start.15 = (bf16[128,512]{1,0:T(8,128)(2,1)S(1)}, bf16[128,512]{1,0:T(8,128)(2,1)S(1)}, u32[]{:S(2)}, u32[]{:S(2)}) collective-permute-start(bf16[128,512]{1,0:T(8,128)(2,1)S(1)} %copy-done.5), channel_id=1, source_target_pairs={{0,64},{1,65},{16,80},{17,81},{32,96},{33,97},{48,112},{49,113},{6... | collective-permute-start | bytes 393224 | tf_op jit(solution)/shard_map/ppermute | solution.py:35
  69.2 0.0 copy-done.4
  69.2 1.3 %collective-permute-start.16 = (bf16[128,512]{1,0:T(8,128)(2,1)S(1)}, bf16[128,512]{1,0:T(8,128)(2,1)S(1)}, u32[]{:S(2)}, u32[]{:S(2)}) collective-permute-start(bf16[128,512]{1,0:T(8,128)(2,1)S(1)} %copy-done.4), channel_id=1, source_target_pairs={{0,80},{1,49},{16,96},{17,65},{32,112},{33,81},{48,0},{49,97},{64,... | collective-permute-start | bytes 393224 | tf_op jit(solution)/shard_map/ppermute | solution.py:35
  70.5 3.1 %collective-permute-start.17 = (bf16[128,512]{1,0:T(8,128)(2,1)}, bf16[128,512]{1,0:T(8,128)(2,1)S(1)}, u32[]{:S(2)}, u32[]{:S(2)}) collective-permute-start(bf16[128,512]{1,0:T(8,128)(2,1)} %get-tuple-element.49), channel_id=1, source_target_pairs={{0,48},{1,81},{16,64},{17,97},{32,80},{33,113},{48,96},{49,1},{64,... | collective-permute-start | bytes 393224 | tf_op jit(solution)/shard_map/ppermute | solution.py:35
  73.6 0.1 collective-permute-start.18
  73.7 3.5 %collective-permute-start.19 = (bf16[128,512]{1,0:T(8,128)(2,1)S(1)}, bf16[128,512]{1,0:T(8,128)(2,1)S(1)}, u32[]{:S(2)}, u32[]{:S(2)}) collective-permute-start(bf16[128,512]{1,0:T(8,128)(2,1)S(1)} %copy-done.3), channel_id=1, source_target_pairs={{0,32},{1,97},{16,48},{17,113},{32,64},{33,1},{48,80},{49,17},{64,... | collective-permute-start | bytes 393224 | tf_op jit(solution)/shard_map/ppermute | solution.py:35
  77.2 0.0 collective-permute-done.15
  77.2 2.7 %collective-permute-start.20 = (bf16[128,512]{1,0:T(8,128)(2,1)S(1)}, bf16[128,512]{1,0:T(8,128)(2,1)S(1)}, u32[]{:S(2)}, u32[]{:S(2)}) collective-permute-start(bf16[128,512]{1,0:T(8,128)(2,1)S(1)} %copy-done.2), channel_id=1, source_target_pairs={{0,112},{1,17},{16,0},{17,33},{32,16},{33,49},{48,32},{49,65},{64,... | collective-permute-start | bytes 393224 | tf_op jit(solution)/shard_map/ppermute | solution.py:35
  79.9 2.6 %collective-permute-done.16 = bf16[128,512]{1,0:T(8,128)(2,1)S(1)} collective-permute-done((bf16[128,512]{1,0:T(8,128)(2,1)S(1)}, bf16[128,512]{1,0:T(8,128)(2,1)S(1)}, u32[]{:S(2)}, u32[]{:S(2)}) %collective-permute-start.16) | collective-permute-done | bytes 131104 | tf_op jit(solution)/shard_map/ppermute | solution.py:35
  82.5 0.0 copy-done.1
  82.5 0.0 collective-permute-start.21
  82.5 16.3 %all-to-all-done.parts = bf16[16,256,256]{2,1,0:T(8,128)(2,1)S(1)} async-done(((bf16[16,256,256]{2,1,0:T(8,128)(2,1)}), bf16[16,256,256]{2,1,0:T(8,128)(2,1)S(1)}, u32[]{:S(2)}, u32[]{:S(2)}) %all-to-all-start) | async-done | bytes 2097184 | tf_op jit(solution)/shard_map/all_to_all | solution.py:291
  98.8 0.8 shard_map.55
  99.6 0.0 collective-permute-done.17
  99.6 1.4 %collective-permute-start.22 = (f32[128,256]{1,0:T(8,128)S(1)}, f32[128,256]{1,0:T(8,128)S(1)}, u32[]{:S(2)}, u32[]{:S(2)}) collective-permute-start(f32[128,256]{1,0:T(8,128)S(1)} %get-tuple-element.57), channel_id=1, source_target_pairs={{0,1},{1,0},{2,3},{3,2},{4,5},{5,4},{6,7},{7,6},{8,9},{9,8},{10,11... | collective-permute-start | bytes 393224 | tf_op jit(solution)/shard_map/ppermute | solution.py:39
  101.0 0.0 collective-permute-done.18
  101.0 0.0 collective-permute-done.19
  101.1 0.0 collective-permute-done.20
  101.1 0.0 collective-permute-done.21
  101.1 0.9 multiply_bitcast_fusion
  101.9 0.1 collective-permute-done.22.received
  102.0 1.4 %shard_map.56 = f32[4,128,128]{2,1,0:T(8,128)} custom-call(s32[4]{0:T(128)S(1)} %pad_add_fusion.position, f32[128,256]{1,0:T(8,128)S(1)} %get-tuple-element.56.keep, f32[128,256]{1,0:T(8,128)S(1)} %collective-permute-done.22.received), custom_call_target="tpu_custom_call" | custom-call | bytes 2097152 | tf_op jit(solution)/shard_map/pallas_call | solution.py:299
  (15 shorter events, 0.2 us)
Async XLA Ops:
  3.1 4.3 %collective-permute-start = (bf16[1,144,512]{2,1,0:T(8,128)(2,1)S(1)}, bf16[1,144,512]{2,1,0:T(8,128)(2,1)S(1)}, u32[]{:S(2)}, u32[]{:S(2)}) collective-permute-start(bf16[1,144,512]{2,1,0:T(8,128)(2,1)S(1)} %get-tuple-element.30), channel_id=1, source_target_pairs={{0,1},{1,0},{2,3},{3,2},{4,5},{5,4},{6,7},{7,6},{8,9},{9,8},{10,11... | collective-permute-start | bytes 442376 | tf_op jit(solution)/shard_map/ppermute | solution.py:39
  7.4 10.0 %collective-permute-start.2 = (bf16[2,144,512]{2,1,0:T(8,128)(2,1)S(1)}, bf16[2,144,512]{2,1,0:T(8,128)(2,1)S(1)}, u32[]{:S(2)}, u32[]{:S(2)}) collective-permute-start(bf16[2,144,512]{2,1,0:T(8,128)(2,1)S(1)} %constant_dynamic-update-slice_fusion.chip), channel_id=1, source_target_pairs={{0,32},{1,97},{16,48},{17,113},{32,64},{33,1},{48,80},{49,17},{64,... | collective-permute-start | bytes 884744 | tf_op jit(solution)/shard_map/ppermute | solution.py:35
  11.8 10.8 %collective-permute-start.1 = (bf16[2,144,512]{2,1,0:T(8,128)(2,1)S(1)}, bf16[2,144,512]{2,1,0:T(8,128)(2,1)S(1)}, u32[]{:S(2)}, u32[]{:S(2)}) collective-permute-start(bf16[2,144,512]{2,1,0:T(8,128)(2,1)S(1)} %constant_dynamic-update-slice_fusion.chip), channel_id=1, source_target_pairs={{0,16},{1,113},{16,32},{17,1},{32,48},{33,17},{48,64},{49,33},{64,... | collective-permute-start | bytes 884744 | tf_op jit(solution)/shard_map/ppermute | solution.py:35
  12.5 10.6 %collective-permute-start.7 = (bf16[4,128,512]{2,1,0:T(8,128)(2,1)S(1)}, bf16[4,128,512]{2,1,0:T(8,128)(2,1)S(1)}, u32[]{:S(2)}, u32[]{:S(2)}) collective-permute-start(bf16[4,128,512]{2,1,0:T(8,128)(2,1)S(1)} %get-tuple-element.31.v0), channel_id=1, source_target_pairs={{0,4},{1,13},{4,8},{5,1},{8,12},{9,5},{12,0},{13,9},{2,6},{3,15},{... | collective-permute-start | bytes 1572872 | tf_op jit(solution)/shard_map/ppermute | solution.py:35
  17.4 9.0 %collective-permute-start.3 = (bf16[2,144,512]{2,1,0:T(8,128)(2,1)S(1)}, bf16[2,144,512]{2,1,0:T(8,128)(2,1)S(1)}, u32[]{:S(2)}, u32[]{:S(2)}) collective-permute-start(bf16[2,144,512]{2,1,0:T(8,128)(2,1)S(1)} %collective-permute-done.2), channel_id=1, source_target_pairs={{0,16},{1,113},{16,32},{17,1},{32,48},{33,17},{48,64},{49,33},{64,... | collective-permute-start | bytes 884744 | tf_op jit(solution)/shard_map/ppermute | solution.py:35
  21.9 6.8 %collective-permute-start.4 = (bf16[1,144,512]{2,1,0:T(8,128)(2,1)S(1)}, bf16[1,144,512]{2,1,0:T(8,128)(2,1)S(1)}, u32[]{:S(2)}, u32[]{:S(2)}) collective-permute-start(bf16[1,144,512]{2,1,0:T(8,128)(2,1)S(1)} %slice.20), channel_id=1, source_target_pairs={{0,32},{1,97},{16,48},{17,113},{32,64},{33,1},{48,80},{49,17},{64,... | collective-permute-start | bytes 442376 | tf_op jit(solution)/shard_map/ppermute | solution.py:35
  22.7 19.2 %collective-permute-start.5 = (bf16[4,144,512]{2,1,0:T(8,128)(2,1)S(1)}, bf16[4,144,512]{2,1,0:T(8,128)(2,1)S(1)}, u32[]{:S(2)}, u32[]{:S(2)}) collective-permute-start(bf16[4,144,512]{2,1,0:T(8,128)(2,1)S(1)} %constant_dynamic-update-slice_fusion.2.near), channel_id=1, source_target_pairs={{0,1},{1,0},{2,3},{3,2},{4,5},{5,4},{6,7},{7,6},{8,9},{9,8},{10,11... | collective-permute-start | bytes 1769480 | tf_op jit(solution)/shard_map/ppermute | solution.py:39
  23.2 16.4 %collective-permute-start.11 = (bf16[4,128,512]{2,1,0:T(8,128)(2,1)S(1)}, bf16[4,128,512]{2,1,0:T(8,128)(2,1)S(1)}, u32[]{:S(2)}, u32[]{:S(2)}) collective-permute-start(bf16[4,128,512]{2,1,0:T(8,128)(2,1)S(1)} %collective-permute-done.7.v1), channel_id=1, source_target_pairs={{0,128},{1,131},{128,2},{129,1},{2,130},{3,129},{130,0},{131,3},{4... | collective-permute-start | bytes 1572872 | tf_op jit(solution)/shard_map/ppermute | solution.py:35
  28.8 13.1 %collective-permute-start.6 = (bf16[3,144,512]{2,1,0:T(8,128)(2,1)S(1)}, bf16[3,144,512]{2,1,0:T(8,128)(2,1)S(1)}, u32[]{:S(2)}, u32[]{:S(2)}) collective-permute-start(bf16[3,144,512]{2,1,0:T(8,128)(2,1)S(1)} %constant_dynamic-update-slice_fusion.4.rest), channel_id=1, source_target_pairs={{0,1},{1,0},{2,3},{3,2},{4,5},{5,4},{6,7},{7,6},{8,9},{9,8},{10,11... | collective-permute-start | bytes 1327112 | tf_op jit(solution)/shard_map/ppermute | solution.py:39
  31.0 6.1 %collective-permute-start.8 = (bf16[2,128,512]{2,1,0:T(8,128)(2,1)S(1)}, bf16[2,128,512]{2,1,0:T(8,128)(2,1)S(1)}, u32[]{:S(2)}, u32[]{:S(2)}) collective-permute-start(bf16[2,128,512]{2,1,0:T(8,128)(2,1)S(1)} %get-tuple-element.59), channel_id=1, source_target_pairs={{0,4},{1,13},{4,8},{5,1},{8,12},{9,5},{12,0},{13,9},{2,6},{3,15},{... | collective-permute-start | bytes 786440 | tf_op jit(solution)/shard_map/ppermute | solution.py:35
  33.8 6.4 %collective-permute-start.9 = (bf16[2,128,512]{2,1,0:T(8,128)(2,1)S(1)}, bf16[2,128,512]{2,1,0:T(8,128)(2,1)S(1)}, u32[]{:S(2)}, u32[]{:S(2)}) collective-permute-start(bf16[2,128,512]{2,1,0:T(8,128)(2,1)S(1)} %get-tuple-element.58), channel_id=1, source_target_pairs={{0,1},{1,0},{2,3},{3,2},{4,5},{5,4},{6,7},{7,6},{8,9},{9,8},{10,11... | collective-permute-start | bytes 786440 | tf_op jit(solution)/shard_map/ppermute | solution.py:39
  37.1 9.4 %collective-permute-start.10 = (bf16[2,128,512]{2,1,0:T(8,128)(2,1)S(1)}, bf16[2,128,512]{2,1,0:T(8,128)(2,1)S(1)}, u32[]{:S(2)}, u32[]{:S(2)}) collective-permute-start(bf16[2,128,512]{2,1,0:T(8,128)(2,1)S(1)} %slice.18), channel_id=1, source_target_pairs={{0,128},{1,131},{128,2},{129,1},{2,130},{3,129},{130,0},{131,3},{4... | collective-permute-start | bytes 786440 | tf_op jit(solution)/shard_map/ppermute | solution.py:35
  39.6 6.9 %collective-permute-start.12 = (bf16[2,128,512]{2,1,0:T(8,128)(2,1)S(1)}, bf16[2,128,512]{2,1,0:T(8,128)(2,1)S(1)}, u32[]{:S(2)}, u32[]{:S(2)}) collective-permute-start(bf16[2,128,512]{2,1,0:T(8,128)(2,1)S(1)} %collective-permute-done.8.v2), channel_id=1, source_target_pairs={{0,128},{1,131},{128,2},{129,1},{2,130},{3,129},{130,0},{131,3},{4... | collective-permute-start | bytes 786440 | tf_op jit(solution)/shard_map/ppermute | solution.py:35
  40.2 6.4 %collective-permute-start.13 = (bf16[2,128,512]{2,1,0:T(8,128)(2,1)S(1)}, bf16[2,128,512]{2,1,0:T(8,128)(2,1)S(1)}, u32[]{:S(2)}, u32[]{:S(2)}) collective-permute-start(bf16[2,128,512]{2,1,0:T(8,128)(2,1)S(1)} %slice.23), channel_id=1, source_target_pairs={{0,1},{1,0},{2,3},{3,2},{4,5},{5,4},{6,7},{7,6},{8,9},{9,8},{10,11... | collective-permute-start | bytes 786440 | tf_op jit(solution)/shard_map/ppermute | solution.py:39
  53.3 6.4 %collective-permute-start.14 = (bf16[1024,512]{1,0:T(8,128)(2,1)}, bf16[1024,512]{1,0:T(8,128)(2,1)S(1)}, u32[]{:S(2)}, u32[]{:S(2)}) collective-permute-start(bf16[1024,512]{1,0:T(8,128)(2,1)} %get-tuple-element.38), channel_id=1, source_target_pairs={{0,1},{1,0},{2,3},{3,2},{4,5},{5,4},{6,7},{7,6},{8,9},{9,8},{10,11... | collective-permute-start | bytes 3145736 | tf_op jit(solution)/shard_map/ppermute | solution.py:39
  60.7 4.5 %copy-start.5 = (bf16[128,512]{1,0:T(8,128)(2,1)S(1)}, bf16[128,512]{1,0:T(8,128)(2,1)}, u32[]{:S(2)}) copy-start(bf16[128,512]{1,0:T(8,128)(2,1)} %get-tuple-element.47) | copy-start | bytes 393220
  60.7 8.4 %copy-start.4 = (bf16[128,512]{1,0:T(8,128)(2,1)S(1)}, bf16[128,512]{1,0:T(8,128)(2,1)}, u32[]{:S(2)}) copy-start(bf16[128,512]{1,0:T(8,128)(2,1)} %get-tuple-element.48) | copy-start | bytes 393220
  60.7 13.0 %copy-start.3 = (bf16[128,512]{1,0:T(8,128)(2,1)S(1)}, bf16[128,512]{1,0:T(8,128)(2,1)}, u32[]{:S(2)}) copy-start(bf16[128,512]{1,0:T(8,128)(2,1)} %get-tuple-element.51) | copy-start | bytes 393220
  60.7 16.5 %copy-start.2 = (bf16[128,512]{1,0:T(8,128)(2,1)S(1)}, bf16[128,512]{1,0:T(8,128)(2,1)}, u32[]{:S(2)}) copy-start(bf16[128,512]{1,0:T(8,128)(2,1)} %get-tuple-element.52) | copy-start | bytes 393220
  60.8 21.8 %copy-start.1 = (bf16[128,512]{1,0:T(8,128)(2,1)S(1)}, bf16[128,512]{1,0:T(8,128)(2,1)}, u32[]{:S(2)}) copy-start(bf16[128,512]{1,0:T(8,128)(2,1)} %get-tuple-element.53) | copy-start | bytes 393220
  60.8 38.0 %all-to-all-start = ((bf16[16,256,256]{2,1,0:T(8,128)(2,1)}), bf16[16,256,256]{2,1,0:T(8,128)(2,1)S(1)}, u32[]{:S(2)}, u32[]{:S(2)}) async-start(bf16[16,256,256]{2,1,0:T(8,128)(2,1)} %shard_map.53), calls=%async_computation | async-start | bytes 4194304 | tf_op jit(solution)/shard_map/all_to_all | solution.py:291
  65.2 35.8 %copy-start = (bf16[128,512]{1,0:T(8,128)(2,1)S(1)}, bf16[128,512]{1,0:T(8,128)(2,1)}, u32[]{:S(2)}) copy-start(bf16[128,512]{1,0:T(8,128)(2,1)} %get-tuple-element.54) | copy-start | bytes 393220
  65.3 12.0 %collective-permute-start.15 = (bf16[128,512]{1,0:T(8,128)(2,1)S(1)}, bf16[128,512]{1,0:T(8,128)(2,1)S(1)}, u32[]{:S(2)}, u32[]{:S(2)}) collective-permute-start(bf16[128,512]{1,0:T(8,128)(2,1)S(1)} %copy-done.5), channel_id=1, source_target_pairs={{0,64},{1,65},{16,80},{17,81},{32,96},{33,97},{48,112},{49,113},{6... | collective-permute-start | bytes 393224 | tf_op jit(solution)/shard_map/ppermute | solution.py:35
  69.2 13.4 %collective-permute-start.16 = (bf16[128,512]{1,0:T(8,128)(2,1)S(1)}, bf16[128,512]{1,0:T(8,128)(2,1)S(1)}, u32[]{:S(2)}, u32[]{:S(2)}) collective-permute-start(bf16[128,512]{1,0:T(8,128)(2,1)S(1)} %copy-done.4), channel_id=1, source_target_pairs={{0,80},{1,49},{16,96},{17,65},{32,112},{33,81},{48,0},{49,97},{64,... | collective-permute-start | bytes 393224 | tf_op jit(solution)/shard_map/ppermute | solution.py:35
  70.5 29.1 %collective-permute-start.17 = (bf16[128,512]{1,0:T(8,128)(2,1)}, bf16[128,512]{1,0:T(8,128)(2,1)S(1)}, u32[]{:S(2)}, u32[]{:S(2)}) collective-permute-start(bf16[128,512]{1,0:T(8,128)(2,1)} %get-tuple-element.49), channel_id=1, source_target_pairs={{0,48},{1,81},{16,64},{17,97},{32,80},{33,113},{48,96},{49,1},{64,... | collective-permute-start | bytes 393224 | tf_op jit(solution)/shard_map/ppermute | solution.py:35
  73.6 27.4 %collective-permute-start.18 = (bf16[128,512]{1,0:T(8,128)(2,1)}, bf16[128,512]{1,0:T(8,128)(2,1)S(1)}, u32[]{:S(2)}, u32[]{:S(2)}) collective-permute-start(bf16[128,512]{1,0:T(8,128)(2,1)} %get-tuple-element.50), channel_id=1, source_target_pairs={{0,96},{1,33},{16,112},{17,49},{32,0},{33,65},{48,16},{49,81},{64,... | collective-permute-start | bytes 393224 | tf_op jit(solution)/shard_map/ppermute | solution.py:35
  73.7 27.3 %collective-permute-start.19 = (bf16[128,512]{1,0:T(8,128)(2,1)S(1)}, bf16[128,512]{1,0:T(8,128)(2,1)S(1)}, u32[]{:S(2)}, u32[]{:S(2)}) collective-permute-start(bf16[128,512]{1,0:T(8,128)(2,1)S(1)} %copy-done.3), channel_id=1, source_target_pairs={{0,32},{1,97},{16,48},{17,113},{32,64},{33,1},{48,80},{49,17},{64,... | collective-permute-start | bytes 393224 | tf_op jit(solution)/shard_map/ppermute | solution.py:35
  77.2 23.8 %collective-permute-start.20 = (bf16[128,512]{1,0:T(8,128)(2,1)S(1)}, bf16[128,512]{1,0:T(8,128)(2,1)S(1)}, u32[]{:S(2)}, u32[]{:S(2)}) collective-permute-start(bf16[128,512]{1,0:T(8,128)(2,1)S(1)} %copy-done.2), channel_id=1, source_target_pairs={{0,112},{1,17},{16,0},{17,33},{32,16},{33,49},{48,32},{49,65},{64,... | collective-permute-start | bytes 393224 | tf_op jit(solution)/shard_map/ppermute | solution.py:35
  82.5 18.5 %collective-permute-start.21 = (bf16[128,512]{1,0:T(8,128)(2,1)S(1)}, bf16[128,512]{1,0:T(8,128)(2,1)S(1)}, u32[]{:S(2)}, u32[]{:S(2)}) collective-permute-start(bf16[128,512]{1,0:T(8,128)(2,1)S(1)} %copy-done.1), channel_id=1, source_target_pairs={{0,16},{1,113},{16,32},{17,1},{32,48},{33,17},{48,64},{49,33},{64,... | collective-permute-start | bytes 393224 | tf_op jit(solution)/shard_map/ppermute | solution.py:35
  99.6 2.4 %collective-permute-start.22 = (f32[128,256]{1,0:T(8,128)S(1)}, f32[128,256]{1,0:T(8,128)S(1)}, u32[]{:S(2)}, u32[]{:S(2)}) collective-permute-start(f32[128,256]{1,0:T(8,128)S(1)} %get-tuple-element.57), channel_id=1, source_target_pairs={{0,1},{1,0},{2,3},{3,2},{4,5},{5,4},{6,7},{7,6},{8,9},{9,8},{10,11... | collective-permute-start | bytes 393224 | tf_op jit(solution)/shard_map/ppermute | solution.py:39
where the time goes:
time: 104 us; the launch traced here: 103 us
  starting transfers between devices  52.1 us (50%)
  waiting for transfers between devices  28.6 us (28%)
  Pallas kernels  20.1 us (19%)
  between operations  1.52 us (1%)
    ppermute x16, starting transfers between devices, opposed(): return lax.ppermute(block, names, route)  36 us
    all_to_all x1, waiting for transfers between devices, step(): grad = lax.all_to_all(grad, PLANE, 0, 0, tiled=True)  16.3 us
    ppermute x7, starting transfers between devices, swap(): return lax.ppermute(block, 'core', [(0, 1), (1, 0)])  11.7 us
    ppermute x16, waiting for transfers between devices, opposed(): return lax.ppermute(block, names, route)  11.2 us
    pallas_call x1, Pallas kernels, step(): call(second, (pltpu.VMEM((2 * zs * o, half * o), BF16), pltpu.VMEM((zs *...  6.74 us
    pallas_call x1, Pallas kernels, step(): call(first, (pltpu.VMEM((2 * zs * o, half * o), BF16), pltpu.VMEM((zs, m,...  4.56 us
    all_to_all x1, starting transfers between devices, step(): grad = lax.all_to_all(grad, PLANE, 0, 0, tiled=True)  4.46 us
    pallas_call x1, Pallas kernels, step(): call(gradient, pltpu.HBM((plane, m // 2, 2 * o), BF16), [SMEM, VMEM, VMEM...  3.76 us
  transfers between devices with their start and end apart: 24, of which 8 were waited for; matrix products, arithmetic and copies ran while one was open for 1% of the time, Pallas kernels for 9%

commit v1 on v0

--- a/solution.py
+++ b/solution.py
@@ -14,9 +14,11 @@
 HBM = pl.BlockSpec(memory_space=pltpu.HBM)
 SMEM = pl.BlockSpec(memory_space=pltpu.SMEM)
 EXTRA = 16
-MINE = ((0, 0), (1, 0), (1, 2), (2, 0), (2, 2), (3, 1), (3, 3), (4, 1))
-THEIRS = ((0, 1), (3, 0), (3, 2), (4, 0), (4, 2), (1, 1), (1, 3), (2, 1))
-OFFSETS = (0, 1, 2, 3, 4, -1, -2, -3)
+EARLY_MINE = ((0, 0), (1, 0), (1, 2), (3, 1), (3, 3))
+EARLY_THEIRS = ((0, 1), (3, 0), (3, 2), (1, 1), (1, 3))
+LATE_MINE = ((2, 0), (2, 2), (4, 1))
+LATE_THEIRS = ((4, 0), (4, 2), (2, 1))
+OFFSETS = (0, 1, 2, -1, -2, 3, 4, -3)
 
 
 def opposed(block, axis, distance):
@@ -81,16 +83,14 @@
             vectors[(2 * g + j) * o : (2 * g + j + 1) * o, :] = group[j]
 
 
-def multiply(vectors, walkers, exch, scaled=None):
-    o = walkers[0].shape[1] - EXTRA
-    count = vectors.shape[0] // o
+def multiply(vectors, walkers, places, exch, base=0, scaled=None):
+    o = vectors.shape[0] // 8
     quad = 4
-    places = MINE + THEIRS
     for i in range(len(places) // 2):
         pair = places[2 * i : 2 * i + 2]
         blocks = [walkers[a][k, :o, :] for a, k in pair]
         both = jnp.concatenate(blocks)
-        for q in range(count // quad):
+        for q in range(2):
             part = lax.dot_general(
                 vectors[q * quad * o : (q + 1) * quad * o, :],
                 both,
@@ -99,23 +99,25 @@
             ).astype(BF16)
             for g in range(quad):
                 for w in range(2):
-                    exch[
-                        (2 * i + w) * o : (2 * i + w + 1) * o, (q * quad + g) * o : (q * quad + g + 1) * o
-                    ] = part[g * o : (g + 1) * o, w * o : (w + 1) * o]
+                    row = base + (2 * i + w) * o
+                    exch[row : row + o, (q * quad + g) * o : (q * quad + g + 1) * o] = part[
+                        g * o : (g + 1) * o, w * o : (w + 1) * o
+                    ]
         if scaled is not None:
             for w, (a, k) in enumerate(pair):
                 weight = jnp.sum(walkers[a][k, o:, :].astype(F32), axis=0, keepdims=True)
                 scaled[i, :, w * o : (w + 1) * o] = (blocks[w].astype(F32) * weight).astype(BF16).T
 
 
-def reduce_walkers(scaled, exch, store):
-    pairs, m, two = scaled.shape
+def reduce_walkers(terms, store):
+    scaled, _, exch, _ = terms[0]
+    _, m, two = scaled.shape
     width = 2 * two
     for c in range(exch.shape[1] // width):
         acc = jnp.zeros((m, width), F32)
-        for i in range(pairs):
+        for scaled, i, exch, row in terms:
             acc += jnp.dot(
-                scaled[i], exch[i * two : (i + 1) * two, c * width : (c + 1) * width], preferred_element_type=F32
+                scaled[i], exch[row : row + two, c * width : (c + 1) * width], preferred_element_type=F32
             )
         acc = acc.astype(BF16)
         for s in range(width // two):
@@ -123,69 +125,129 @@
                 store(c * (width // two) + s, h, acc[h * m // 2 : (h + 1) * m // 2, s * two : (s + 1) * two])
 
 
-def first(chip, near, rest, w1, w2, v0, v1, v2, v3, exch, scaled, vectors, grad):
+def terms_of(scaled, exch, base=0):
+    two = scaled.shape[2]
+    return [(scaled, i, exch, base + i * two) for i in range(scaled.shape[0])]
+
+
+def started(*copies):
+    for copy in copies:
+        copy.start()
+    return list(copies)
+
+
+def early(chip, near, w1, v0, v1, v2, v3, exch, scaled, vectors, kept_exch, kept_vectors, sems):
     collect((v0, v1, v2, v3), vectors)
-    multiply(vectors, (chip, near, rest, w1, w2), exch, scaled)
+    copies = started(pltpu.make_async_copy(vectors, kept_vectors, sems.at[0]))
+    multiply(vectors, {0: chip, 1: near, 3: w1}, EARLY_MINE + EARLY_THEIRS, exch, scaled=scaled)
+    rows = kept_exch.shape[0]
+    copies += started(pltpu.make_async_copy(exch.at[pl.ds(0, rows)], kept_exch, sems.at[1]))
+    for copy in copies:
+        copy.wait()
+
+
+def first(rest, w2, exch0, scaled0, vectors, exch, scaled, grad, kept_exch, sems):
+    multiply(vectors, {2: rest, 4: w2}, LATE_MINE + LATE_THEIRS, exch, scaled=scaled)
+    rows = kept_exch.shape[0]
+    copies = started(pltpu.make_async_copy(exch.at[pl.ds(0, rows)], kept_exch, sems.at[0]))
 
     def store(group, h, block):
         grad[2 * group + h] = block
 
-    reduce_walkers(scaled, exch, store)
-
-
-def second(chip, near, rest, w1, w2, v0, v1, v2, v3, exch0, vectors0, exch, cot_mine, cot_theirs, vectors, cot, sems):
+    reduce_walkers(terms_of(scaled0, exch0) + terms_of(scaled, exch), store)
+    for copy in copies:
+        copy.wait()
+
+
+def second(
+    chip, near, rest, w1, w2, v0, v1, v2, v3, exch0, exch1, vectors0, exch, cot_theirs, kept_exch, kept_vectors, vectors, cot, sems
+):
+    o = vectors.shape[0] // 8
     collect((v0, v1, v2, v3), vectors)
-    multiply(vectors, (chip, near, rest, w1, w2), exch)
-    half = cot_mine.shape[0]
-    run = 512
-    stores = []
-    for r in range(2 * half // run):
-        base = (half + r * run) % (2 * half)
-        rows = slice(base, base + run)
-        part = jnp.dot(exch0[rows, :], vectors0[...], preferred_element_type=F32)
-        part += jnp.dot(exch[rows, :], vectors[...], preferred_element_type=F32)
-        if base >= half:
-            target = slice(base - half, base - half + run)
-            cot[target, :] = part.astype(BF16)
-            stores.append(pltpu.make_async_copy(cot.at[target], cot_theirs.at[target], sems.at[r]))
-            stores[-1].start()
-        else:
-            cot_mine[rows, :] = part
-    for copy in stores:
-        copy.wait()
-
-
-def gradient(position, scaled, exch, grad0, grad, staged, sems):
+    places = EARLY_MINE + EARLY_THEIRS + LATE_MINE + LATE_THEIRS
+    multiply(vectors, (chip, near, rest, w1, w2), places, exch)
+    split, total_early = len(EARLY_MINE) * o, 2 * len(EARLY_MINE) * o
+    count = len(LATE_MINE) * o
+    copies = started(
+        pltpu.make_async_copy(vectors, kept_vectors, sems.at[0]),
+        pltpu.make_async_copy(exch.at[pl.ds(0, split)], kept_exch.at[pl.ds(0, split)], sems.at[1]),
+        pltpu.make_async_copy(exch.at[pl.ds(total_early, count)], kept_exch.at[pl.ds(split, count)], sems.at[2]),
+    )
+    for r, (own, row, size, base) in enumerate(((exch0, split, split, 0), (exch1, count, count, total_early))):
+        target = slice(r * split, r * split + size)
+        part = jnp.dot(own[row : row + size, :], vectors0[...], preferred_element_type=F32)
+        part += jnp.dot(exch[base + row : base + row + size, :], vectors[...], preferred_element_type=F32)
+        cot[target, :] = part.astype(BF16)
+        copies += started(pltpu.make_async_copy(cot.at[target], cot_theirs.at[target], sems.at[3 + r]))
+    for copy in copies:
+        copy.wait()
+
+
+def gradient(position, scaled0, scaled1, exch, grad0, grad, staged, sems):
     core, column, y, rows = position[0], position[1], position[2], position[3]
     step = 2 * core - 1
     places = [lax.rem(y + d + rows, rows) for d in (0, step, 2, -step)]
     copies = []
     for g, place in enumerate(places):
         target = grad.at[pl.ds((column * rows + place) * 2, 2)]
-        copies.append(pltpu.make_async_copy(grad0.at[pl.ds(2 * g, 2)], target, sems.at[g]))
-        copies[-1].start()
+        copies += started(pltpu.make_async_copy(grad0.at[pl.ds(2 * g, 2)], target, sems.at[g]))
 
     def store(group, h, block):
         staged[2 * group + h] = block
         if h == 1:
             target = grad.at[pl.ds(((1 - column) * rows + places[group]) * 2, 2)]
-            copies.append(pltpu.make_async_copy(staged.at[pl.ds(2 * group, 2)], target, sems.at[4 + group]))
-            copies[-1].start()
-
-    reduce_walkers(scaled, exch, store)
-    for copy in copies:
-        copy.wait()
-
-
-def join(cot_mine, returned, *refs):
-    outs, (staged, sems) = refs[:-2], refs[-2:]
+            copies.extend(started(pltpu.make_async_copy(staged.at[pl.ds(2 * group, 2)], target, sems.at[4 + group])))
+
+    base = scaled0.shape[0] * scaled0.shape[2]
+    reduce_walkers(terms_of(scaled0, exch) + terms_of(scaled1, exch, base), store)
+    for copy in copies:
+        copy.wait()
+
+
+def finish(kept_early, kept_late, vectors0, kept1, vectors1, returned, *refs):
+    outs, (exch, vectors, staged, sems, out_sems) = refs[:-5], refs[-5:]
     o = outs[0].shape[0]
+    early_rows = kept_early.shape[0]
+    cuts = [0, 2 * o, 4 * o, 6 * o, 8 * o]
+    pieces = []
+    for lo, hi in zip(cuts, cuts[1:]):
+        piece = []
+        for source, at, a, b in (
+            (kept_early, 0, lo, min(hi, early_rows)),
+            (kept_late, early_rows, max(lo, early_rows), hi),
+        ):
+            if a < b:
+                k = len(pieces) * 3 + len(piece)
+                piece.append(
+                    pltpu.make_async_copy(
+                        source.at[pl.ds(a - at, b - a)], exch.at[0, pl.ds(a, b - a)], sems.at[2 + k]
+                    )
+                )
+        k = len(pieces) * 3 + 2
+        other = pltpu.make_async_copy(kept1.at[pl.ds(lo, hi - lo)], exch.at[1, pl.ds(lo, hi - lo)], sems.at[2 + k])
+        pieces.append((piece, other))
+    load0 = started(pltpu.make_async_copy(vectors0, vectors.at[0], sems.at[0]))[0]
+    started(*pieces[0][0])
+    load1 = started(pltpu.make_async_copy(vectors1, vectors.at[1], sems.at[1]))[0]
+    pieces[0][1].start()
+    for piece, other in pieces[1:]:
+        started(*piece, other)
+    load0.wait()
     stores = []
-    for k, out in enumerate(outs):
-        rows = slice(k * o, (k + 1) * o)
-        staged[k] = (cot_mine[rows, :] + returned[rows, :].astype(F32)).astype(BF16)
-        stores.append(pltpu.make_async_copy(staged.at[k], out, sems.at[k]))
-        stores[-1].start()
+    for r, (piece, other) in enumerate(pieces):
+        lo, hi = cuts[r], cuts[r + 1]
+        for copy in piece:
+            copy.wait()
+        part = jnp.dot(exch[0, lo:hi, :], vectors[0], preferred_element_type=F32)
+        if r == 0:
+            load1.wait()
+        other.wait()
+        part += jnp.dot(exch[1, lo:hi, :], vectors[1], preferred_element_type=F32)
+        part += returned[lo:hi, :].astype(F32)
+        for w in range((hi - lo) // o):
+            k = lo // o + w
+            staged[k] = part[w * o : (w + 1) * o, :].astype(BF16)
+            stores += started(pltpu.make_async_copy(staged.at[k], outs[k], out_sems.at[k]))
     for copy in stores:
         copy.wait()
 
@@ -245,55 +307,86 @@
 
     half = plane // 2
     pair_flops = 2 * o * o * m
-    exch0, scaled, vectors0, grad0 = call(
+    ne, nl = len(EARLY_MINE), len(LATE_MINE)
+    exch0, scaled0, vectors0, kept_early, kept_vectors0 = call(
+        early,
+        (
+            pltpu.VMEM((2 * ne * o, half * o), BF16),
+            pltpu.VMEM((ne, m, 2 * o), BF16),
+            pltpu.VMEM((half * o, m), BF16),
+            pltpu.HBM((ne * o, half * o), BF16),
+            pltpu.HBM((half * o, m), BF16),
+        ),
+        [VMEM] * 7,
+        20,
+        flops=2 * ne * half * pair_flops,
+        scratch=[dma((2,))],
+        out_specs=(VMEM,) * 3 + (HBM,) * 2,
+    )(chip, near, w1, ordered, y1, y2, y3)
+
+    exch1, scaled1, grad0, kept_late = call(
         first,
         (
-            pltpu.VMEM((2 * zs * o, half * o), BF16),
-            pltpu.VMEM((zs, m, 2 * o), BF16),
-            pltpu.VMEM((half * o, m), BF16),
+            pltpu.VMEM((2 * nl * o, half * o), BF16),
+            pltpu.VMEM((nl, m, 2 * o), BF16),
             pltpu.VMEM((half, m // 2, 2 * o), BF16),
+            pltpu.HBM((nl * o, half * o), BF16),
         ),
-        [VMEM] * 9,
+        [VMEM] * 5,
         24,
         flops=2 * zs * plane * pair_flops,
-    )(chip, near, rest, w1, w2, ordered, y1, y2, y3)
-
-    exch1, cot_mine, cot_theirs = call(
+        scratch=[dma((1,))],
+        out_specs=(VMEM,) * 3 + (HBM,),
+    )(rest, w2, exch0, scaled0, vectors0)
+
+    exch, cot_theirs, kept1, kept_vectors1 = call(
         second,
-        (pltpu.VMEM((2 * zs * o, half * o), BF16), pltpu.VMEM((zs * o, m), F32), pltpu.HBM((zs * o, m), BF16)),
-        [VMEM] * 11,
+        (
+            pltpu.VMEM((2 * zs * o, half * o), BF16),
+            pltpu.HBM((zs * o, m), BF16),
+            pltpu.HBM((zs * o, half * o), BF16),
+            pltpu.HBM((half * o, m), BF16),
+        ),
+        [VMEM] * 12,
         32,
-        flops=3 * zs * plane * pair_flops,
-        scratch=[pltpu.VMEM((half * o, m), BF16), pltpu.VMEM((zs * o, m), BF16), dma((4,))],
-        out_specs=(VMEM, VMEM, HBM),
-    )(chip, near, rest, w1, w2, x0, x1, x2, x3, exch0, vectors0)
+        flops=2 * zs * plane * pair_flops,
+        scratch=[pltpu.VMEM((half * o, m), BF16), pltpu.VMEM((zs * o, m), BF16), dma((5,))],
+        out_specs=(VMEM,) + (HBM,) * 3,
+    )(chip, near, rest, w1, w2, x0, x1, x2, x3, exch0, exch1, vectors0)
     returned = swap(cot_theirs)
 
     grad = call(
         gradient,
         pltpu.HBM((plane, m // 2, 2 * o), BF16),
-        [SMEM, VMEM, VMEM, VMEM],
+        [SMEM] + [VMEM] * 4,
         24,
         flops=zs * plane * pair_flops,
         scratch=[pltpu.VMEM((half, m // 2, 2 * o), BF16), dma((8,))],
         out_specs=HBM,
-    )(position, scaled, exch1, grad0)
-
+    )(position, scaled0, scaled1, exch, grad0)
+
+    grad = lax.all_to_all(grad, PLANE, 0, 0, tiled=True)
     sums = call(
-        join,
+        finish,
         tuple(pltpu.HBM((o, m), BF16) for _ in range(zs)),
-        [VMEM] * 2,
-        16,
-        scratch=[pltpu.VMEM((zs, o, m), BF16), dma((zs,))],
+        [HBM] * 5 + [VMEM],
+        24,
+        flops=zs * plane * pair_flops,
+        scratch=[
+            pltpu.VMEM((2, zs * o, half * o), BF16),
+            pltpu.VMEM((2, half * o, m), BF16),
+            pltpu.VMEM((zs, o, m), BF16),
+            dma((14,)),
+            dma((zs,)),
+        ],
         out_specs=(HBM,) * zs,
-    )(cot_mine, returned)
-    grad, *sums = lax.optimization_barrier((grad, *sums))
-    grad = lax.all_to_all(grad, PLANE, 0, 0, tiled=True)
+    )(*(hold(x) for x in (kept_early, kept_late, kept_vectors0, kept1, kept_vectors1)), returned)
     cot = None
     for k, block in sorted(zip(OFFSETS, sums), key=lambda kb: -abs(kb[0])):
         part = (block if k == 0 else opposed(block, "z", -k)).astype(F32)
         cot = part if cot is None else cot + part
-    green_cot = (-weight[0] * cot)[None]
+    minus = -weight[0]
+    green_cot = (minus * cot)[None]
 
     keep, send = call(total, (shape((m // 4, 2 * o), F32),) * 2, [SMEM, VMEM], 16)(position, grad)
     chol_grad = call(place, shape((4, o, m // 4), F32), [SMEM, VMEM, VMEM], 16)(position, keep, swap(send))

time: 104 us -> 102 us (0.981)
  waiting for transfers between devices: 28.6 us -> 18.4 us
  Pallas kernels: 20.1 us -> 25.2 us
  starting transfers between devices: 52.1 us -> 55.1 us
    all_to_all x1, waiting for transfers between devices: 16.3 us -> 7.16 us  [step(): grad = lax.all_to_all(grad, PLANE, 0, 0, tiled=True)]
    pallas_call x4 -> x5, Pallas kernels: 16.1 us -> 21.2 us  [the longest x1 5.89 us: step(): call(finish, tuple((pltpu.HBM((o, m), BF16) for _ in range(zs))), [HBM] *...]
    ppermute x16, starting transfers between devices: 36 us -> 40.6 us  [opposed(): return lax.ppermute(block, names, route)]
    ppermute x16, waiting for transfers between devices: 11.2 us -> 7.89 us  [opposed(): return lax.ppermute(block, names, route)]
    ppermute x7, starting transfers between devices: 11.7 us -> 9.04 us  [swap(): return lax.ppermute(block, 'core', [(0, 1), (1, 0)])]
    ppermute x7, waiting for transfers between devices: 1.11 us -> 3.36 us  [swap(): return lax.ppermute(block, 'core', [(0, 1), (1, 0)])]
  transfers between devices with their start and end apart: 24 -> 24, of which waited for: 8 -> 10; matrix products, arithmetic and copies ran while one was open for 1% -> 1% of each run, Pallas kernels for 9% -> 13%
where the time goes in v1:
time: 102 us; the launch traced here: 101 us
  starting transfers between devices  55.1 us (54%)
  Pallas kernels  25.2 us (25%)
  waiting for transfers between devices  18.4 us (18%)
  between operations  1.48 us (1%)
    ppermute x16, starting transfers between devices, opposed(): return lax.ppermute(block, names, route)  40.6 us
    ppermute x7, starting transfers between devices, swap(): return lax.ppermute(block, 'core', [(0, 1), (1, 0)])  9.04 us
    ppermute x16, waiting for transfers between devices, opposed(): return lax.ppermute(block, names, route)  7.89 us
    all_to_all x1, waiting for transfers between devices, step(): grad = lax.all_to_all(grad, PLANE, 0, 0, tiled=True)  7.16 us
    pallas_call x1, Pallas kernels, step(): call(finish, tuple((pltpu.HBM((o, m), BF16) for _ in range(zs))), [HBM] *...  5.89 us
    all_to_all x1, starting transfers between devices, step(): grad = lax.all_to_all(grad, PLANE, 0, 0, tiled=True)  5.42 us
    pallas_call x1, Pallas kernels, step(): call(second, (pltpu.VMEM((2 * zs * o, half * o), BF16), pltpu.HBM((zs * o...  5.4 us
    pallas_call x1, Pallas kernels, step(): call(gradient, pltpu.HBM((plane, m // 2, 2 * o), BF16), [SMEM] + [VMEM] *...  3.76 us
  transfers between devices with their start and end apart: 24, of which 10 were waited for; matrix products, arithmetic and copies ran while one was open for 1% of the time, Pallas kernels for 13%

profile of v1, /device:TPU:1, one launch (start us, length us, event | category | flops | bytes accessed | tf_op | source)
XLA Modules:
  0.0 101.3 jit_solution(2388536797982632716)
XLA Ops:
  1.3 0.1 pad_add_fusion.position
  1.4 1.7 %shard_map.50 = (bf16[1,144,512]{2,1,0:T(8,128)(2,1)S(1)}, bf16[4,128,512]{2,1,0:T(8,128)(2,1)S(1)}) custom-call(s32[4]{0:T(128)S(1)} %pad_add_fusion.position, f32[1]{0:T(128)S(6)} %copy.8.weight, bf16[1,128,512]{2,1,0:T(8,128)(2,1)} %green.1, bf16[4,128,512]{2,1,0:T(8,128)(2,1)} %vectors.1), custom_call_target="tpu_custom_call" | custom-call | bytes 2097152 | tf_op jit(solution)/shard_map/pallas_call | solution.py:283
  3.1 3.3 %collective-permute-start = (bf16[1,144,512]{2,1,0:T(8,128)(2,1)S(1)}, bf16[1,144,512]{2,1,0:T(8,128)(2,1)S(1)}, u32[]{:S(2)}, u32[]{:S(2)}) collective-permute-start(bf16[1,144,512]{2,1,0:T(8,128)(2,1)S(1)} %get-tuple-element.27), channel_id=1, source_target_pairs={{0,1},{1,0},{2,3},{3,2},{4,5},{5,4},{6,7},{7,6},{8,9},{9,8},{10,11... | collective-permute-start | bytes 442376 | tf_op jit(solution)/shard_map/ppermute | solution.py:41
  6.4 1.0 collective-permute-done
  7.4 4.4 %collective-permute-start.2 = (bf16[2,144,512]{2,1,0:T(8,128)(2,1)S(1)}, bf16[2,144,512]{2,1,0:T(8,128)(2,1)S(1)}, u32[]{:S(2)}, u32[]{:S(2)}) collective-permute-start(bf16[2,144,512]{2,1,0:T(8,128)(2,1)S(1)} %constant_dynamic-update-slice_fusion.chip), channel_id=1, source_target_pairs={{0,32},{1,97},{16,48},{17,113},{32,64},{33,1},{48,80},{49,17},{64,... | collective-permute-start | bytes 884744 | tf_op jit(solution)/shard_map/ppermute | solution.py:37
  11.8 0.7 collective-permute-start.1
  12.5 2.7 %collective-permute-start.4 = (bf16[4,128,512]{2,1,0:T(8,128)(2,1)S(1)}, bf16[4,128,512]{2,1,0:T(8,128)(2,1)S(1)}, u32[]{:S(2)}, u32[]{:S(2)}) collective-permute-start(bf16[4,128,512]{2,1,0:T(8,128)(2,1)S(1)} %get-tuple-element.28.v0), channel_id=1, source_target_pairs={{0,4},{1,13},{4,8},{5,1},{8,12},{9,5},{12,0},{13,9},{2,6},{3,15},{... | collective-permute-start | bytes 1572872 | tf_op jit(solution)/shard_map/ppermute | solution.py:37
  15.3 2.2 %collective-permute-done.2 = bf16[2,144,512]{2,1,0:T(8,128)(2,1)S(1)} collective-permute-done((bf16[2,144,512]{2,1,0:T(8,128)(2,1)S(1)}, bf16[2,144,512]{2,1,0:T(8,128)(2,1)S(1)}, u32[]{:S(2)}, u32[]{:S(2)}) %collective-permute-start.2) | collective-permute-done | bytes 294944 | tf_op jit(solution)/shard_map/ppermute | solution.py:37
  17.4 4.5 %collective-permute-start.7 = (bf16[2,144,512]{2,1,0:T(8,128)(2,1)S(1)}, bf16[2,144,512]{2,1,0:T(8,128)(2,1)S(1)}, u32[]{:S(2)}, u32[]{:S(2)}) collective-permute-start(bf16[2,144,512]{2,1,0:T(8,128)(2,1)S(1)} %collective-permute-done.2), channel_id=1, source_target_pairs={{0,16},{1,113},{16,32},{17,1},{32,48},{33,17},{48,64},{49,33},{64,... | collective-permute-start | bytes 884744 | tf_op jit(solution)/shard_map/ppermute | solution.py:37
  21.9 0.7 collective-permute-start.8
  22.6 0.0 collective-permute-done.1
  22.7 0.5 collective-permute-start.3
  23.2 0.0 collective-permute-done.4.v1
  23.2 2.5 %collective-permute-start.11 = (bf16[4,128,512]{2,1,0:T(8,128)(2,1)S(1)}, bf16[4,128,512]{2,1,0:T(8,128)(2,1)S(1)}, u32[]{:S(2)}, u32[]{:S(2)}) collective-permute-start(bf16[4,128,512]{2,1,0:T(8,128)(2,1)S(1)} %collective-permute-done.4.v1), channel_id=1, source_target_pairs={{0,128},{1,131},{128,2},{129,1},{2,130},{3,129},{130,0},{131,3},{4... | collective-permute-start | bytes 1572872 | tf_op jit(solution)/shard_map/ppermute | solution.py:37
  25.7 0.8 collective-permute-done.7
  26.4 2.4 %collective-permute-done.8 = bf16[1,144,512]{2,1,0:T(8,128)(2,1)S(1)} collective-permute-done((bf16[1,144,512]{2,1,0:T(8,128)(2,1)S(1)}, bf16[1,144,512]{2,1,0:T(8,128)(2,1)S(1)}, u32[]{:S(2)}, u32[]{:S(2)}) %collective-permute-start.8) | collective-permute-done | bytes 147488 | tf_op jit(solution)/shard_map/ppermute | solution.py:37
  28.8 2.1 %collective-permute-start.9 = (bf16[3,144,512]{2,1,0:T(8,128)(2,1)S(1)}, bf16[3,144,512]{2,1,0:T(8,128)(2,1)S(1)}, u32[]{:S(2)}, u32[]{:S(2)}) collective-permute-start(bf16[3,144,512]{2,1,0:T(8,128)(2,1)S(1)} %constant_dynamic-update-slice_fusion.4.rest), channel_id=1, source_target_pairs={{0,1},{1,0},{2,3},{3,2},{4,5},{5,4},{6,7},{7,6},{8,9},{9,8},{10,11... | collective-permute-start | bytes 1327112 | tf_op jit(solution)/shard_map/ppermute | solution.py:41
  31.0 0.1 collective-permute-start.6
  31.1 2.8 %collective-permute-start.5 = (bf16[2,128,512]{2,1,0:T(8,128)(2,1)S(1)}, bf16[2,128,512]{2,1,0:T(8,128)(2,1)S(1)}, u32[]{:S(2)}, u32[]{:S(2)}) collective-permute-start(bf16[2,128,512]{2,1,0:T(8,128)(2,1)S(1)} %get-tuple-element.53), channel_id=1, source_target_pairs={{0,4},{1,13},{4,8},{5,1},{8,12},{9,5},{12,0},{13,9},{2,6},{3,15},{... | collective-permute-start | bytes 786440 | tf_op jit(solution)/shard_map/ppermute | solution.py:37
  33.9 0.0 collective-permute-done.6.v3
  33.9 2.6 %collective-permute-start.10 = (bf16[2,128,512]{2,1,0:T(8,128)(2,1)S(1)}, bf16[2,128,512]{2,1,0:T(8,128)(2,1)S(1)}, u32[]{:S(2)}, u32[]{:S(2)}) collective-permute-start(bf16[2,128,512]{2,1,0:T(8,128)(2,1)S(1)} %slice.18), channel_id=1, source_target_pairs={{0,128},{1,131},{128,2},{129,1},{2,130},{3,129},{130,0},{131,3},{4... | collective-permute-start | bytes 786440 | tf_op jit(solution)/shard_map/ppermute | solution.py:37
  36.5 0.7 collective-permute-done.5.v2
  37.2 2.5 %collective-permute-start.12 = (bf16[2,128,512]{2,1,0:T(8,128)(2,1)S(1)}, bf16[2,128,512]{2,1,0:T(8,128)(2,1)S(1)}, u32[]{:S(2)}, u32[]{:S(2)}) collective-permute-start(bf16[2,128,512]{2,1,0:T(8,128)(2,1)S(1)} %collective-permute-done.5.v2), channel_id=1, source_target_pairs={{0,128},{1,131},{128,2},{129,1},{2,130},{3,129},{130,0},{131,3},{4... | collective-permute-start | bytes 786440 | tf_op jit(solution)/shard_map/ppermute | solution.py:37
  39.7 0.0 collective-permute-done.3.w1
  39.7 3.0 %shard_map.51 = (bf16[1280,1024]{1,0:T(8,128)(2,1)S(1)}, bf16[5,512,256]{2,1,0:T(8,128)(2,1)S(1)}, bf16[1024,512]{1,0:T(8,128)(2,1)S(1)}, bf16[640,1024]{1,0:T(8,128)(2,1)}, bf16[1024,512]{1,0:T(8,128)(2,1)}) custom-call(bf16[2,144,512]{2,1,0:T(8,128)(2,1)S(1)} %constant_dynamic-update-slice_fusion.chip, ...), custom_call_target="tpu_custom_call" | custom-call | flops 1342177280 | bytes 2097152 | tf_op jit(solution)/shard_map/pallas_call | solution.py:311
  42.7 0.0 collective-permute-done.11.v1
  42.7 1.2 %collective-permute-start.13 = (bf16[2,128,512]{2,1,0:T(8,128)(2,1)S(1)}, bf16[2,128,512]{2,1,0:T(8,128)(2,1)S(1)}, u32[]{:S(2)}, u32[]{:S(2)}) collective-permute-start(bf16[2,128,512]{2,1,0:T(8,128)(2,1)S(1)} %slice.23), channel_id=1, source_target_pairs={{0,1},{1,0},{2,3},{3,2},{4,5},{5,4},{6,7},{7,6},{8,9},{9,8},{10,11... | collective-permute-start | bytes 786440 | tf_op jit(solution)/shard_map/ppermute | solution.py:41
  43.9 0.0 collective-permute-done.9.w2
  43.9 3.2 %shard_map.52 = (bf16[768,1024]{1,0:T(8,128)(2,1)S(1)}, bf16[3,512,256]{2,1,0:T(8,128)(2,1)S(1)}, bf16[8,256,256]{2,1,0:T(8,128)(2,1)S(1)}, bf16[384,1024]{1,0:T(8,128)(2,1)}) custom-call(bf16[3,144,512]{2,1,0:T(8,128)(2,1)S(1)} %constant_dynamic-update-slice_fusion.4.rest, bf16[3,144,512]{2,1,0:T(8,128)(2,1)S(1)} %collective-permute-done.9.w2, ...), custom_call_target="tpu_custom_call" | custom-call | flops 4294967296 | bytes 2097152 | tf_op jit(solution)/shard_map/pallas_call | solution.py:327
  47.1 0.0 collective-permute-done.10.v0
  47.2 0.0 collective-permute-done.12.v2
  47.2 0.0 collective-permute-done.13.v3
  47.2 5.4 %shard_map.53 = (bf16[2048,1024]{1,0:T(8,128)(2,1)S(1)}, bf16[1024,512]{1,0:T(8,128)(2,1)}, bf16[1024,1024]{1,0:T(8,128)(2,1)}, bf16[1024,512]{1,0:T(8,128)(2,1)}) custom-call(bf16[2,144,512]{2,1,0:T(8,128)(2,1)S(1)} %constant_dynamic-update-slice_fusion.chip, bf16[4,144,512]{2,1,0:T(8,128)(2,1)S(1)} %constant_dynamic-update-slice_fusion.2.near, ...), custom_call_target="tpu_custom_call" | custom-call | flops 4294967296 | bytes 2097152 | tf_op jit(solution)/shard_map/pallas_call | solution.py:342
  52.6 3.8 %shard_map.55 = bf16[16,256,256]{2,1,0:T(8,128)(2,1)} custom-call(s32[4]{0:T(128)S(1)} %pad_add_fusion.position, bf16[5,512,256]{2,1,0:T(8,128)(2,1)S(1)} %get-tuple-element.31.scaled0, bf16[3,512,256]{2,1,0:T(8,128)(2,1)S(1)} %get-tuple-element.47.scaled1, bf16[2048,1024]{1,0:T(8,128)(2,1)S(1)} %get-tuple-element.48.exch, ...), custom_call_target="tpu_custom_call" | custom-call | flops 2147483648 | bytes 2097152 | tf_op jit(solution)/shard_map/pallas_call | solution.py:358
  56.4 0.0 copy-start.1
  56.4 5.4 %all-to-all-start = ((bf16[16,256,256]{2,1,0:T(8,128)(2,1)}), bf16[16,256,256]{2,1,0:T(8,128)(2,1)S(1)}, u32[]{:S(2)}, u32[]{:S(2)}) async-start(bf16[16,256,256]{2,1,0:T(8,128)(2,1)} %shard_map.55), calls=%async_computation | async-start | bytes 4194304 | tf_op jit(solution)/shard_map/all_to_all | solution.py:368
  61.8 0.0 copy-done.1
  61.8 0.4 collective-permute-start.14
  62.2 2.4 %collective-permute-done.14.returned = bf16[1024,512]{1,0:T(8,128)(2,1)S(1)} collective-permute-done((bf16[1024,512]{1,0:T(8,128)(2,1)S(1)}, bf16[1024,512]{1,0:T(8,128)(2,1)S(1)}, u32[]{:S(2)}, u32[]{:S(2)}) %collective-permute-start.14) | collective-permute-done | bytes 1048608 | tf_op jit(solution)/shard_map/ppermute | solution.py:41
  64.5 5.9 %shard_map.54 = (bf16[128,512]{1,0:T(8,128)(2,1)}, bf16[128,512]{1,0:T(8,128)(2,1)}, bf16[128,512]{1,0:T(8,128)(2,1)}, bf16[128,512]{1,0:T(8,128)(2,1)}, bf16[12...) custom-call(bf16[640,1024]{1,0:T(8,128)(2,1)} %get-tuple-element.29.kept_earl, ...), custom_call_target="tpu_custom_call" | custom-call | flops 2147483648 | bytes 2097152 | tf_op jit(solution)/shard_map/pallas_call | solution.py:369
  70.4 0.0 copy-start
  70.5 3.9 %collective-permute-start.15 = (bf16[128,512]{1,0:T(8,128)(2,1)}, bf16[128,512]{1,0:T(8,128)(2,1)S(1)}, u32[]{:S(2)}, u32[]{:S(2)}) collective-permute-start(bf16[128,512]{1,0:T(8,128)(2,1)} %get-tuple-element.39), channel_id=1, source_target_pairs={{0,64},{1,65},{16,80},{17,81},{32,96},{33,97},{48,112},{49,113},{6... | collective-permute-start | bytes 393224 | tf_op jit(solution)/shard_map/ppermute | solution.py:37
  74.4 1.3 %collective-permute-start.16 = (bf16[128,512]{1,0:T(8,128)(2,1)}, bf16[128,512]{1,0:T(8,128)(2,1)S(1)}, u32[]{:S(2)}, u32[]{:S(2)}) collective-permute-start(bf16[128,512]{1,0:T(8,128)(2,1)} %get-tuple-element.40), channel_id=1, source_target_pairs={{0,80},{1,49},{16,96},{17,65},{32,112},{33,81},{48,0},{49,97},{64,... | collective-permute-start | bytes 393224 | tf_op jit(solution)/shard_map/ppermute | solution.py:37
  75.7 3.2 %collective-permute-start.17 = (bf16[128,512]{1,0:T(8,128)(2,1)}, bf16[128,512]{1,0:T(8,128)(2,1)S(1)}, u32[]{:S(2)}, u32[]{:S(2)}) collective-permute-start(bf16[128,512]{1,0:T(8,128)(2,1)} %get-tuple-element.41), channel_id=1, source_target_pairs={{0,48},{1,81},{16,64},{17,97},{32,80},{33,113},{48,96},{49,1},{64,... | collective-permute-start | bytes 393224 | tf_op jit(solution)/shard_map/ppermute | solution.py:37
  78.8 0.0 collective-permute-start.18
  78.8 3.6 %collective-permute-start.19 = (bf16[128,512]{1,0:T(8,128)(2,1)}, bf16[128,512]{1,0:T(8,128)(2,1)S(1)}, u32[]{:S(2)}, u32[]{:S(2)}) collective-permute-start(bf16[128,512]{1,0:T(8,128)(2,1)} %get-tuple-element.43), channel_id=1, source_target_pairs={{0,32},{1,97},{16,48},{17,113},{32,64},{33,1},{48,80},{49,17},{64,... | collective-permute-start | bytes 393224 | tf_op jit(solution)/shard_map/ppermute | solution.py:37
  82.4 0.6 collective-permute-done.15
  83.0 2.1 %collective-permute-start.20 = (bf16[128,512]{1,0:T(8,128)(2,1)}, bf16[128,512]{1,0:T(8,128)(2,1)S(1)}, u32[]{:S(2)}, u32[]{:S(2)}) collective-permute-start(bf16[128,512]{1,0:T(8,128)(2,1)} %get-tuple-element.44), channel_id=1, source_target_pairs={{0,112},{1,17},{16,0},{17,33},{32,16},{33,49},{48,32},{49,65},{64,... | collective-permute-start | bytes 393224 | tf_op jit(solution)/shard_map/ppermute | solution.py:37
  85.1 0.5 collective-permute-done.16
  85.6 3.2 %collective-permute-start.21 = (bf16[128,512]{1,0:T(8,128)(2,1)}, bf16[128,512]{1,0:T(8,128)(2,1)S(1)}, u32[]{:S(2)}, u32[]{:S(2)}) collective-permute-start(bf16[128,512]{1,0:T(8,128)(2,1)} %get-tuple-element.45), channel_id=1, source_target_pairs={{0,16},{1,113},{16,32},{17,1},{32,48},{33,17},{48,64},{49,33},{64,... | collective-permute-start | bytes 393224 | tf_op jit(solution)/shard_map/ppermute | solution.py:37
  88.8 7.2 %all-to-all-done.parts = bf16[16,256,256]{2,1,0:T(8,128)(2,1)S(1)} async-done(((bf16[16,256,256]{2,1,0:T(8,128)(2,1)}), bf16[16,256,256]{2,1,0:T(8,128)(2,1)S(1)}, u32[]{:S(2)}, u32[]{:S(2)}) %all-to-all-start) | async-done | bytes 2097184 | tf_op jit(solution)/shard_map/all_to_all | solution.py:368
  95.9 0.8 shard_map.56
  96.8 0.0 collective-permute-done.17
  96.8 1.4 %collective-permute-start.22 = (f32[128,256]{1,0:T(8,128)S(1)}, f32[128,256]{1,0:T(8,128)S(1)}, u32[]{:S(2)}, u32[]{:S(2)}) collective-permute-start(f32[128,256]{1,0:T(8,128)S(1)} %get-tuple-element.51), channel_id=1, source_target_pairs={{0,1},{1,0},{2,3},{3,2},{4,5},{5,4},{6,7},{7,6},{8,9},{9,8},{10,11... | collective-permute-start | bytes 393224 | tf_op jit(solution)/shard_map/ppermute | solution.py:41
  98.2 0.0 collective-permute-done.18
  98.2 0.0 collective-permute-done.19
  98.2 0.0 collective-permute-done.20
  98.2 0.8 collective-permute-done.21
  99.1 0.0 copy-done
  99.1 0.8 multiply_bitcast_fusion
  99.9 0.0 collective-permute-done.22.received
  99.9 1.4 %shard_map.57 = f32[4,128,128]{2,1,0:T(8,128)} custom-call(s32[4]{0:T(128)S(1)} %pad_add_fusion.position, f32[128,256]{1,0:T(8,128)S(1)} %get-tuple-element.50.keep, f32[128,256]{1,0:T(8,128)S(1)} %collective-permute-done.22.received), custom_call_target="tpu_custom_call" | custom-call | bytes 2097152 | tf_op jit(solution)/shard_map/pallas_call | solution.py:392
  (10 shorter events, 0.2 us)
Async XLA Ops:
  3.1 4.3 %collective-permute-start = (bf16[1,144,512]{2,1,0:T(8,128)(2,1)S(1)}, bf16[1,144,512]{2,1,0:T(8,128)(2,1)S(1)}, u32[]{:S(2)}, u32[]{:S(2)}) collective-permute-start(bf16[1,144,512]{2,1,0:T(8,128)(2,1)S(1)} %get-tuple-element.27), channel_id=1, source_target_pairs={{0,1},{1,0},{2,3},{3,2},{4,5},{5,4},{6,7},{7,6},{8,9},{9,8},{10,11... | collective-permute-start | bytes 442376 | tf_op jit(solution)/shard_map/ppermute | solution.py:41
  7.4 10.0 %collective-permute-start.2 = (bf16[2,144,512]{2,1,0:T(8,128)(2,1)S(1)}, bf16[2,144,512]{2,1,0:T(8,128)(2,1)S(1)}, u32[]{:S(2)}, u32[]{:S(2)}) collective-permute-start(bf16[2,144,512]{2,1,0:T(8,128)(2,1)S(1)} %constant_dynamic-update-slice_fusion.chip), channel_id=1, source_target_pairs={{0,32},{1,97},{16,48},{17,113},{32,64},{33,1},{48,80},{49,17},{64,... | collective-permute-start | bytes 884744 | tf_op jit(solution)/shard_map/ppermute | solution.py:37
  11.8 10.8 %collective-permute-start.1 = (bf16[2,144,512]{2,1,0:T(8,128)(2,1)S(1)}, bf16[2,144,512]{2,1,0:T(8,128)(2,1)S(1)}, u32[]{:S(2)}, u32[]{:S(2)}) collective-permute-start(bf16[2,144,512]{2,1,0:T(8,128)(2,1)S(1)} %constant_dynamic-update-slice_fusion.chip), channel_id=1, source_target_pairs={{0,16},{1,113},{16,32},{17,1},{32,48},{33,17},{48,64},{49,33},{64,... | collective-permute-start | bytes 884744 | tf_op jit(solution)/shard_map/ppermute | solution.py:37
  12.5 10.6 %collective-permute-start.4 = (bf16[4,128,512]{2,1,0:T(8,128)(2,1)S(1)}, bf16[4,128,512]{2,1,0:T(8,128)(2,1)S(1)}, u32[]{:S(2)}, u32[]{:S(2)}) collective-permute-start(bf16[4,128,512]{2,1,0:T(8,128)(2,1)S(1)} %get-tuple-element.28.v0), channel_id=1, source_target_pairs={{0,4},{1,13},{4,8},{5,1},{8,12},{9,5},{12,0},{13,9},{2,6},{3,15},{... | collective-permute-start | bytes 1572872 | tf_op jit(solution)/shard_map/ppermute | solution.py:37
  17.4 9.0 %collective-permute-start.7 = (bf16[2,144,512]{2,1,0:T(8,128)(2,1)S(1)}, bf16[2,144,512]{2,1,0:T(8,128)(2,1)S(1)}, u32[]{:S(2)}, u32[]{:S(2)}) collective-permute-start(bf16[2,144,512]{2,1,0:T(8,128)(2,1)S(1)} %collective-permute-done.2), channel_id=1, source_target_pairs={{0,16},{1,113},{16,32},{17,1},{32,48},{33,17},{48,64},{49,33},{64,... | collective-permute-start | bytes 884744 | tf_op jit(solution)/shard_map/ppermute | solution.py:37
  21.9 6.8 %collective-permute-start.8 = (bf16[1,144,512]{2,1,0:T(8,128)(2,1)S(1)}, bf16[1,144,512]{2,1,0:T(8,128)(2,1)S(1)}, u32[]{:S(2)}, u32[]{:S(2)}) collective-permute-start(bf16[1,144,512]{2,1,0:T(8,128)(2,1)S(1)} %slice.22), channel_id=1, source_target_pairs={{0,32},{1,97},{16,48},{17,113},{32,64},{33,1},{48,80},{49,17},{64,... | collective-permute-start | bytes 442376 | tf_op jit(solution)/shard_map/ppermute | solution.py:37
  22.7 17.0 %collective-permute-start.3 = (bf16[4,144,512]{2,1,0:T(8,128)(2,1)S(1)}, bf16[4,144,512]{2,1,0:T(8,128)(2,1)S(1)}, u32[]{:S(2)}, u32[]{:S(2)}) collective-permute-start(bf16[4,144,512]{2,1,0:T(8,128)(2,1)S(1)} %constant_dynamic-update-slice_fusion.2.near), channel_id=1, source_target_pairs={{0,1},{1,0},{2,3},{3,2},{4,5},{5,4},{6,7},{7,6},{8,9},{9,8},{10,11... | collective-permute-start | bytes 1769480 | tf_op jit(solution)/shard_map/ppermute | solution.py:41
  23.2 19.5 %collective-permute-start.11 = (bf16[4,128,512]{2,1,0:T(8,128)(2,1)S(1)}, bf16[4,128,512]{2,1,0:T(8,128)(2,1)S(1)}, u32[]{:S(2)}, u32[]{:S(2)}) collective-permute-start(bf16[4,128,512]{2,1,0:T(8,128)(2,1)S(1)} %collective-permute-done.4.v1), channel_id=1, source_target_pairs={{0,128},{1,131},{128,2},{129,1},{2,130},{3,129},{130,0},{131,3},{4... | collective-permute-start | bytes 1572872 | tf_op jit(solution)/shard_map/ppermute | solution.py:37
  28.8 15.1 %collective-permute-start.9 = (bf16[3,144,512]{2,1,0:T(8,128)(2,1)S(1)}, bf16[3,144,512]{2,1,0:T(8,128)(2,1)S(1)}, u32[]{:S(2)}, u32[]{:S(2)}) collective-permute-start(bf16[3,144,512]{2,1,0:T(8,128)(2,1)S(1)} %constant_dynamic-update-slice_fusion.4.rest), channel_id=1, source_target_pairs={{0,1},{1,0},{2,3},{3,2},{4,5},{5,4},{6,7},{7,6},{8,9},{9,8},{10,11... | collective-permute-start | bytes 1327112 | tf_op jit(solution)/shard_map/ppermute | solution.py:41
  31.0 2.9 %collective-permute-start.6 = (bf16[2,128,512]{2,1,0:T(8,128)(2,1)S(1)}, bf16[2,128,512]{2,1,0:T(8,128)(2,1)S(1)}, u32[]{:S(2)}, u32[]{:S(2)}) collective-permute-start(bf16[2,128,512]{2,1,0:T(8,128)(2,1)S(1)} %get-tuple-element.52), channel_id=1, source_target_pairs={{0,1},{1,0},{2,3},{3,2},{4,5},{5,4},{6,7},{7,6},{8,9},{9,8},{10,11... | collective-permute-start | bytes 786440 | tf_op jit(solution)/shard_map/ppermute | solution.py:41
  31.1 6.1 %collective-permute-start.5 = (bf16[2,128,512]{2,1,0:T(8,128)(2,1)S(1)}, bf16[2,128,512]{2,1,0:T(8,128)(2,1)S(1)}, u32[]{:S(2)}, u32[]{:S(2)}) collective-permute-start(bf16[2,128,512]{2,1,0:T(8,128)(2,1)S(1)} %get-tuple-element.53), channel_id=1, source_target_pairs={{0,4},{1,13},{4,8},{5,1},{8,12},{9,5},{12,0},{13,9},{2,6},{3,15},{... | collective-permute-start | bytes 786440 | tf_op jit(solution)/shard_map/ppermute | solution.py:37
  33.9 13.2 %collective-permute-start.10 = (bf16[2,128,512]{2,1,0:T(8,128)(2,1)S(1)}, bf16[2,128,512]{2,1,0:T(8,128)(2,1)S(1)}, u32[]{:S(2)}, u32[]{:S(2)}) collective-permute-start(bf16[2,128,512]{2,1,0:T(8,128)(2,1)S(1)} %slice.18), channel_id=1, source_target_pairs={{0,128},{1,131},{128,2},{129,1},{2,130},{3,129},{130,0},{131,3},{4... | collective-permute-start | bytes 786440 | tf_op jit(solution)/shard_map/ppermute | solution.py:37
  37.2 10.0 %collective-permute-start.12 = (bf16[2,128,512]{2,1,0:T(8,128)(2,1)S(1)}, bf16[2,128,512]{2,1,0:T(8,128)(2,1)S(1)}, u32[]{:S(2)}, u32[]{:S(2)}) collective-permute-start(bf16[2,128,512]{2,1,0:T(8,128)(2,1)S(1)} %collective-permute-done.5.v2), channel_id=1, source_target_pairs={{0,128},{1,131},{128,2},{129,1},{2,130},{3,129},{130,0},{131,3},{4... | collective-permute-start | bytes 786440 | tf_op jit(solution)/shard_map/ppermute | solution.py:37
  42.7 4.5 %collective-permute-start.13 = (bf16[2,128,512]{2,1,0:T(8,128)(2,1)S(1)}, bf16[2,128,512]{2,1,0:T(8,128)(2,1)S(1)}, u32[]{:S(2)}, u32[]{:S(2)}) collective-permute-start(bf16[2,128,512]{2,1,0:T(8,128)(2,1)S(1)} %slice.23), channel_id=1, source_target_pairs={{0,1},{1,0},{2,3},{3,2},{4,5},{5,4},{6,7},{7,6},{8,9},{9,8},{10,11... | collective-permute-start | bytes 786440 | tf_op jit(solution)/shard_map/ppermute | solution.py:41
  56.4 5.4 %copy-start.1 = (bf16[1024,512]{1,0:T(8,128)(2,1)S(1)}, bf16[1024,512]{1,0:T(8,128)(2,1)}, u32[]{:S(2)}) copy-start(bf16[1024,512]{1,0:T(8,128)(2,1)} %get-tuple-element.38) | copy-start | bytes 3145732
  56.4 39.6 %all-to-all-start = ((bf16[16,256,256]{2,1,0:T(8,128)(2,1)}), bf16[16,256,256]{2,1,0:T(8,128)(2,1)S(1)}, u32[]{:S(2)}, u32[]{:S(2)}) async-start(bf16[16,256,256]{2,1,0:T(8,128)(2,1)} %shard_map.55), calls=%async_computation | async-start | bytes 4194304 | tf_op jit(solution)/shard_map/all_to_all | solution.py:368
  61.8 2.7 %collective-permute-start.14 = (bf16[1024,512]{1,0:T(8,128)(2,1)S(1)}, bf16[1024,512]{1,0:T(8,128)(2,1)S(1)}, u32[]{:S(2)}, u32[]{:S(2)}) collective-permute-start(bf16[1024,512]{1,0:T(8,128)(2,1)S(1)} %copy-done.1), channel_id=1, source_target_pairs={{0,1},{1,0},{2,3},{3,2},{4,5},{5,4},{6,7},{7,6},{8,9},{9,8},{10,11... | collective-permute-start | bytes 3145736 | tf_op jit(solution)/shard_map/ppermute | solution.py:41
  70.4 28.6 %copy-start = (bf16[128,512]{1,0:T(8,128)(2,1)S(1)}, bf16[128,512]{1,0:T(8,128)(2,1)}, u32[]{:S(2)}) copy-start(bf16[128,512]{1,0:T(8,128)(2,1)} %get-tuple-element.46) | copy-start | bytes 393220
  70.5 12.5 %collective-permute-start.15 = (bf16[128,512]{1,0:T(8,128)(2,1)}, bf16[128,512]{1,0:T(8,128)(2,1)S(1)}, u32[]{:S(2)}, u32[]{:S(2)}) collective-permute-start(bf16[128,512]{1,0:T(8,128)(2,1)} %get-tuple-element.39), channel_id=1, source_target_pairs={{0,64},{1,65},{16,80},{17,81},{32,96},{33,97},{48,112},{49,113},{6... | collective-permute-start | bytes 393224 | tf_op jit(solution)/shard_map/ppermute | solution.py:37
  74.4 11.2 %collective-permute-start.16 = (bf16[128,512]{1,0:T(8,128)(2,1)}, bf16[128,512]{1,0:T(8,128)(2,1)S(1)}, u32[]{:S(2)}, u32[]{:S(2)}) collective-permute-start(bf16[128,512]{1,0:T(8,128)(2,1)} %get-tuple-element.40), channel_id=1, source_target_pairs={{0,80},{1,49},{16,96},{17,65},{32,112},{33,81},{48,0},{49,97},{64,... | collective-permute-start | bytes 393224 | tf_op jit(solution)/shard_map/ppermute | solution.py:37
  75.7 21.1 %collective-permute-start.17 = (bf16[128,512]{1,0:T(8,128)(2,1)}, bf16[128,512]{1,0:T(8,128)(2,1)S(1)}, u32[]{:S(2)}, u32[]{:S(2)}) collective-permute-start(bf16[128,512]{1,0:T(8,128)(2,1)} %get-tuple-element.41), channel_id=1, source_target_pairs={{0,48},{1,81},{16,64},{17,97},{32,80},{33,113},{48,96},{49,1},{64,... | collective-permute-start | bytes 393224 | tf_op jit(solution)/shard_map/ppermute | solution.py:37
  78.8 19.4 %collective-permute-start.18 = (bf16[128,512]{1,0:T(8,128)(2,1)}, bf16[128,512]{1,0:T(8,128)(2,1)S(1)}, u32[]{:S(2)}, u32[]{:S(2)}) collective-permute-start(bf16[128,512]{1,0:T(8,128)(2,1)} %get-tuple-element.42), channel_id=1, source_target_pairs={{0,96},{1,33},{16,112},{17,49},{32,0},{33,65},{48,16},{49,81},{64,... | collective-permute-start | bytes 393224 | tf_op jit(solution)/shard_map/ppermute | solution.py:37
  78.8 19.4 %collective-permute-start.19 = (bf16[128,512]{1,0:T(8,128)(2,1)}, bf16[128,512]{1,0:T(8,128)(2,1)S(1)}, u32[]{:S(2)}, u32[]{:S(2)}) collective-permute-start(bf16[128,512]{1,0:T(8,128)(2,1)} %get-tuple-element.43), channel_id=1, source_target_pairs={{0,32},{1,97},{16,48},{17,113},{32,64},{33,1},{48,80},{49,17},{64,... | collective-permute-start | bytes 393224 | tf_op jit(solution)/shard_map/ppermute | solution.py:37
  83.0 15.3 %collective-permute-start.20 = (bf16[128,512]{1,0:T(8,128)(2,1)}, bf16[128,512]{1,0:T(8,128)(2,1)S(1)}, u32[]{:S(2)}, u32[]{:S(2)}) collective-permute-start(bf16[128,512]{1,0:T(8,128)(2,1)} %get-tuple-element.44), channel_id=1, source_target_pairs={{0,112},{1,17},{16,0},{17,33},{32,16},{33,49},{48,32},{49,65},{64,... | collective-permute-start | bytes 393224 | tf_op jit(solution)/shard_map/ppermute | solution.py:37
  85.6 13.5 %collective-permute-start.21 = (bf16[128,512]{1,0:T(8,128)(2,1)}, bf16[128,512]{1,0:T(8,128)(2,1)S(1)}, u32[]{:S(2)}, u32[]{:S(2)}) collective-permute-start(bf16[128,512]{1,0:T(8,128)(2,1)} %get-tuple-element.45), channel_id=1, source_target_pairs={{0,16},{1,113},{16,32},{17,1},{32,48},{33,17},{48,64},{49,33},{64,... | collective-permute-start | bytes 393224 | tf_op jit(solution)/shard_map/ppermute | solution.py:37
  96.8 3.1 %collective-permute-start.22 = (f32[128,256]{1,0:T(8,128)S(1)}, f32[128,256]{1,0:T(8,128)S(1)}, u32[]{:S(2)}, u32[]{:S(2)}) collective-permute-start(f32[128,256]{1,0:T(8,128)S(1)} %get-tuple-element.51), channel_id=1, source_target_pairs={{0,1},{1,0},{2,3},{3,2},{4,5},{5,4},{6,7},{7,6},{8,9},{9,8},{10,11... | collective-permute-start | bytes 393224 | tf_op jit(solution)/shard_map/ppermute | solution.py:41

commit v2 on v1

--- a/solution.py
+++ b/solution.py
@@ -112,7 +112,7 @@
 def reduce_walkers(terms, store):
     scaled, _, exch, _ = terms[0]
     _, m, two = scaled.shape
-    width = 2 * two
+    width = two
     for c in range(exch.shape[1] // width):
         acc = jnp.zeros((m, width), F32)
         for scaled, i, exch, row in terms:
@@ -125,9 +125,9 @@
                 store(c * (width // two) + s, h, acc[h * m // 2 : (h + 1) * m // 2, s * two : (s + 1) * two])
 
 
-def terms_of(scaled, exch, base=0):
+def terms_of(scaled, exch):
     two = scaled.shape[2]
-    return [(scaled, i, exch, base + i * two) for i in range(scaled.shape[0])]
+    return [(scaled, i, exch, i * two) for i in range(scaled.shape[0])]
 
 
 def started(*copies):
@@ -159,31 +159,31 @@
         copy.wait()
 
 
-def second(
-    chip, near, rest, w1, w2, v0, v1, v2, v3, exch0, exch1, vectors0, exch, cot_theirs, kept_exch, kept_vectors, vectors, cot, sems
-):
-    o = vectors.shape[0] // 8
+def beyond(chip, near, w1, v0, v1, v2, v3, exch, vectors, kept_exch, kept_vectors, sems):
     collect((v0, v1, v2, v3), vectors)
-    places = EARLY_MINE + EARLY_THEIRS + LATE_MINE + LATE_THEIRS
-    multiply(vectors, (chip, near, rest, w1, w2), places, exch)
-    split, total_early = len(EARLY_MINE) * o, 2 * len(EARLY_MINE) * o
-    count = len(LATE_MINE) * o
-    copies = started(
-        pltpu.make_async_copy(vectors, kept_vectors, sems.at[0]),
-        pltpu.make_async_copy(exch.at[pl.ds(0, split)], kept_exch.at[pl.ds(0, split)], sems.at[1]),
-        pltpu.make_async_copy(exch.at[pl.ds(total_early, count)], kept_exch.at[pl.ds(split, count)], sems.at[2]),
-    )
-    for r, (own, row, size, base) in enumerate(((exch0, split, split, 0), (exch1, count, count, total_early))):
+    copies = started(pltpu.make_async_copy(vectors, kept_vectors, sems.at[0]))
+    multiply(vectors, {0: chip, 1: near, 3: w1}, EARLY_MINE + EARLY_THEIRS, exch)
+    rows = kept_exch.shape[0]
+    copies += started(pltpu.make_async_copy(exch.at[pl.ds(0, rows)], kept_exch, sems.at[1]))
+    for copy in copies:
+        copy.wait()
+
+
+def second(rest, w2, exch0, exch1, exch2, vectors0, vectors1, exch, cot_theirs, kept_exch, cot, sems):
+    multiply(vectors1, {2: rest, 4: w2}, LATE_MINE + LATE_THEIRS, exch)
+    split, count = exch0.shape[0] // 2, exch1.shape[0] // 2
+    copies = started(pltpu.make_async_copy(exch.at[pl.ds(0, count)], kept_exch, sems.at[0]))
+    for r, (own, other, size) in enumerate(((exch0, exch2, split), (exch1, exch, count))):
         target = slice(r * split, r * split + size)
-        part = jnp.dot(own[row : row + size, :], vectors0[...], preferred_element_type=F32)
-        part += jnp.dot(exch[base + row : base + row + size, :], vectors[...], preferred_element_type=F32)
+        part = jnp.dot(own[size : 2 * size, :], vectors0[...], preferred_element_type=F32)
+        part += jnp.dot(other[size : 2 * size, :], vectors1[...], preferred_element_type=F32)
         cot[target, :] = part.astype(BF16)
-        copies += started(pltpu.make_async_copy(cot.at[target], cot_theirs.at[target], sems.at[3 + r]))
-    for copy in copies:
-        copy.wait()
-
-
-def gradient(position, scaled0, scaled1, exch, grad0, grad, staged, sems):
+        copies += started(pltpu.make_async_copy(cot.at[target], cot_theirs.at[target], sems.at[1 + r]))
+    for copy in copies:
+        copy.wait()
+
+
+def gradient(position, scaled0, scaled1, exch0, exch1, grad0, grad, staged, sems):
     core, column, y, rows = position[0], position[1], position[2], position[3]
     step = 2 * core - 1
     places = [lax.rem(y + d + rows, rows) for d in (0, step, 2, -step)]
@@ -198,40 +198,37 @@
             target = grad.at[pl.ds(((1 - column) * rows + places[group]) * 2, 2)]
             copies.extend(started(pltpu.make_async_copy(staged.at[pl.ds(2 * group, 2)], target, sems.at[4 + group])))
 
-    base = scaled0.shape[0] * scaled0.shape[2]
-    reduce_walkers(terms_of(scaled0, exch) + terms_of(scaled1, exch, base), store)
-    for copy in copies:
-        copy.wait()
-
-
-def finish(kept_early, kept_late, vectors0, kept1, vectors1, returned, *refs):
+    reduce_walkers(terms_of(scaled0, exch0) + terms_of(scaled1, exch1), store)
+    for copy in copies:
+        copy.wait()
+
+
+def finish(early0, late0, vectors0, early1, late1, vectors1, returned, *refs):
     outs, (exch, vectors, staged, sems, out_sems) = refs[:-5], refs[-5:]
     o = outs[0].shape[0]
-    early_rows = kept_early.shape[0]
-    cuts = [0, 2 * o, 4 * o, 6 * o, 8 * o]
+    split = early0.shape[0]
+    cuts = [0, 4 * o, 8 * o]
     pieces = []
+    count = 2
     for lo, hi in zip(cuts, cuts[1:]):
-        piece = []
-        for source, at, a, b in (
-            (kept_early, 0, lo, min(hi, early_rows)),
-            (kept_late, early_rows, max(lo, early_rows), hi),
-        ):
-            if a < b:
-                k = len(pieces) * 3 + len(piece)
-                piece.append(
-                    pltpu.make_async_copy(
-                        source.at[pl.ds(a - at, b - a)], exch.at[0, pl.ds(a, b - a)], sems.at[2 + k]
+        both = []
+        for h, (early_rows, late_rows) in enumerate(((early0, late0), (early1, late1))):
+            piece = []
+            for source, at, a, b in ((early_rows, 0, lo, min(hi, split)), (late_rows, split, max(lo, split), hi)):
+                if a < b:
+                    rows = pl.ds(a, b - a)
+                    piece.append(
+                        pltpu.make_async_copy(source.at[pl.ds(a - at, b - a)], exch.at[h, rows], sems.at[count])
                     )
-                )
-        k = len(pieces) * 3 + 2
-        other = pltpu.make_async_copy(kept1.at[pl.ds(lo, hi - lo)], exch.at[1, pl.ds(lo, hi - lo)], sems.at[2 + k])
-        pieces.append((piece, other))
+                    count += 1
+            both.append(piece)
+        pieces.append(both)
     load0 = started(pltpu.make_async_copy(vectors0, vectors.at[0], sems.at[0]))[0]
     started(*pieces[0][0])
     load1 = started(pltpu.make_async_copy(vectors1, vectors.at[1], sems.at[1]))[0]
-    pieces[0][1].start()
+    started(*pieces[0][1])
     for piece, other in pieces[1:]:
-        started(*piece, other)
+        started(*piece, *other)
     load0.wait()
     stores = []
     for r, (piece, other) in enumerate(pieces):
@@ -241,7 +238,8 @@
         part = jnp.dot(exch[0, lo:hi, :], vectors[0], preferred_element_type=F32)
         if r == 0:
             load1.wait()
-        other.wait()
+        for copy in other:
+            copy.wait()
         part += jnp.dot(exch[1, lo:hi, :], vectors[1], preferred_element_type=F32)
         part += returned[lo:hi, :].astype(F32)
         for w in range((hi - lo) // o):
@@ -339,37 +337,51 @@
         out_specs=(VMEM,) * 3 + (HBM,),
     )(rest, w2, exch0, scaled0, vectors0)
 
-    exch, cot_theirs, kept1, kept_vectors1 = call(
+    exch2, vectors1, kept_early1, kept_vectors1 = call(
+        beyond,
+        (
+            pltpu.VMEM((2 * ne * o, half * o), BF16),
+            pltpu.VMEM((half * o, m), BF16),
+            pltpu.HBM((ne * o, half * o), BF16),
+            pltpu.HBM((half * o, m), BF16),
+        ),
+        [VMEM] * 7,
+        20,
+        flops=2 * ne * half * pair_flops,
+        scratch=[dma((2,))],
+        out_specs=(VMEM,) * 2 + (HBM,) * 2,
+    )(chip, near, w1, x0, x1, x2, x3)
+
+    exch3, cot_theirs, kept_late1 = call(
         second,
         (
-            pltpu.VMEM((2 * zs * o, half * o), BF16),
+            pltpu.VMEM((2 * nl * o, half * o), BF16),
             pltpu.HBM((zs * o, m), BF16),
-            pltpu.HBM((zs * o, half * o), BF16),
-            pltpu.HBM((half * o, m), BF16),
+            pltpu.HBM((nl * o, half * o), BF16),
         ),
-        [VMEM] * 12,
-        32,
+        [VMEM] * 7,
+        24,
         flops=2 * zs * plane * pair_flops,
-        scratch=[pltpu.VMEM((half * o, m), BF16), pltpu.VMEM((zs * o, m), BF16), dma((5,))],
-        out_specs=(VMEM,) + (HBM,) * 3,
-    )(chip, near, rest, w1, w2, x0, x1, x2, x3, exch0, exch1, vectors0)
+        scratch=[pltpu.VMEM((zs * o, m), BF16), dma((3,))],
+        out_specs=(VMEM,) + (HBM,) * 2,
+    )(rest, w2, exch0, exch1, exch2, vectors0, vectors1)
     returned = swap(cot_theirs)
 
     grad = call(
         gradient,
         pltpu.HBM((plane, m // 2, 2 * o), BF16),
-        [SMEM] + [VMEM] * 4,
+        [SMEM] + [VMEM] * 5,
         24,
         flops=zs * plane * pair_flops,
         scratch=[pltpu.VMEM((half, m // 2, 2 * o), BF16), dma((8,))],
         out_specs=HBM,
-    )(position, scaled0, scaled1, exch, grad0)
+    )(position, scaled0, scaled1, exch2, exch3, grad0)
 
     grad = lax.all_to_all(grad, PLANE, 0, 0, tiled=True)
     sums = call(
         finish,
         tuple(pltpu.HBM((o, m), BF16) for _ in range(zs)),
-        [HBM] * 5 + [VMEM],
+        [HBM] * 6 + [VMEM],
         24,
         flops=zs * plane * pair_flops,
         scratch=[
@@ -380,7 +392,7 @@
             dma((zs,)),
         ],
         out_specs=(HBM,) * zs,
-    )(*(hold(x) for x in (kept_early, kept_late, kept_vectors0, kept1, kept_vectors1)), returned)
+    )(*(hold(x) for x in (kept_early, kept_late, kept_vectors0, kept_early1, kept_late1, kept_vectors1)), returned)
     cot = None
     for k, block in sorted(zip(OFFSETS, sums), key=lambda kb: -abs(kb[0])):
         part = (block if k == 0 else opposed(block, "z", -k)).astype(F32)

time: 102 us -> 103 us (level)
  Pallas kernels: 25.2 us -> 26.3 us
    pallas_call x1 -> x2, Pallas kernels: 5.4 us -> 6.64 us  [the longest x1 3.99 us: step(): call(second, (pltpu.VMEM((2 * nl * o, half * o), BF16), pltpu.HBM((zs * o...]
  transfers between devices with their start and end apart: 24 -> 24, of which waited for: 10 -> 10; matrix products, arithmetic and copies ran while one was open for 1% -> 1% of each run, Pallas kernels for 13% -> 12%
where the time goes in v2:
time: 103 us; the launch traced here: 102 us
  starting transfers between devices  55.1 us (53%)
  Pallas kernels  26.3 us (26%)
  waiting for transfers between devices  18.4 us (18%)
  between operations  1.49 us (1%)
    ppermute x16, starting transfers between devices, opposed(): return lax.ppermute(block, names, route)  40.7 us
    ppermute x7, starting transfers between devices, swap(): return lax.ppermute(block, 'core', [(0, 1), (1, 0)])  8.93 us
    ppermute x16, waiting for transfers between devices, opposed(): return lax.ppermute(block, names, route)  7.8 us
    all_to_all x1, waiting for transfers between devices, step(): grad = lax.all_to_all(grad, PLANE, 0, 0, tiled=True)  7.28 us
    pallas_call x1, Pallas kernels, step(): call(finish, tuple((pltpu.HBM((o, m), BF16) for _ in range(zs))), [HBM] *...  5.76 us
    all_to_all x1, starting transfers between devices, step(): grad = lax.all_to_all(grad, PLANE, 0, 0, tiled=True)  5.42 us
    pallas_call x1, Pallas kernels, step(): call(second, (pltpu.VMEM((2 * nl * o, half * o), BF16), pltpu.HBM((zs * o...  3.99 us
    pallas_call x1, Pallas kernels, step(): call(gradient, pltpu.HBM((plane, m // 2, 2 * o), BF16), [SMEM] + [VMEM] *...  3.76 us
  transfers between devices with their start and end apart: 24, of which 10 were waited for; matrix products, arithmetic and copies ran while one was open for 1% of the time, Pallas kernels for 12%

profile of v2, /device:TPU:1, one launch (start us, length us, event | category | flops | bytes accessed | tf_op | source)
XLA Modules:
  0.0 102.5 jit_solution(15000887393262203529)
XLA Ops:
  1.3 0.1 pad_add_fusion.position
  1.4 1.7 %shard_map.50 = (bf16[1,144,512]{2,1,0:T(8,128)(2,1)S(1)}, bf16[4,128,512]{2,1,0:T(8,128)(2,1)S(1)}) custom-call(s32[4]{0:T(128)S(1)} %pad_add_fusion.position, f32[1]{0:T(128)S(6)} %copy.8.weight, bf16[1,128,512]{2,1,0:T(8,128)(2,1)} %green.1, bf16[4,128,512]{2,1,0:T(8,128)(2,1)} %vectors.1), custom_call_target="tpu_custom_call" | custom-call | bytes 2097152 | tf_op jit(solution)/shard_map/pallas_call | solution.py:281
  3.1 3.3 %collective-permute-start = (bf16[1,144,512]{2,1,0:T(8,128)(2,1)S(1)}, bf16[1,144,512]{2,1,0:T(8,128)(2,1)S(1)}, u32[]{:S(2)}, u32[]{:S(2)}) collective-permute-start(bf16[1,144,512]{2,1,0:T(8,128)(2,1)S(1)} %get-tuple-element.30), channel_id=1, source_target_pairs={{0,1},{1,0},{2,3},{3,2},{4,5},{5,4},{6,7},{7,6},{8,9},{9,8},{10,11... | collective-permute-start | bytes 442376 | tf_op jit(solution)/shard_map/ppermute | solution.py:41
  6.4 1.0 collective-permute-done
  7.4 4.4 %collective-permute-start.2 = (bf16[2,144,512]{2,1,0:T(8,128)(2,1)S(1)}, bf16[2,144,512]{2,1,0:T(8,128)(2,1)S(1)}, u32[]{:S(2)}, u32[]{:S(2)}) collective-permute-start(bf16[2,144,512]{2,1,0:T(8,128)(2,1)S(1)} %constant_dynamic-update-slice_fusion.chip), channel_id=1, source_target_pairs={{0,32},{1,97},{16,48},{17,113},{32,64},{33,1},{48,80},{49,17},{64,... | collective-permute-start | bytes 884744 | tf_op jit(solution)/shard_map/ppermute | solution.py:37
  11.8 0.7 collective-permute-start.1
  12.5 2.7 %collective-permute-start.4 = (bf16[4,128,512]{2,1,0:T(8,128)(2,1)S(1)}, bf16[4,128,512]{2,1,0:T(8,128)(2,1)S(1)}, u32[]{:S(2)}, u32[]{:S(2)}) collective-permute-start(bf16[4,128,512]{2,1,0:T(8,128)(2,1)S(1)} %get-tuple-element.31.v0), channel_id=1, source_target_pairs={{0,4},{1,13},{4,8},{5,1},{8,12},{9,5},{12,0},{13,9},{2,6},{3,15},{... | collective-permute-start | bytes 1572872 | tf_op jit(solution)/shard_map/ppermute | solution.py:37
  15.3 2.2 %collective-permute-done.2 = bf16[2,144,512]{2,1,0:T(8,128)(2,1)S(1)} collective-permute-done((bf16[2,144,512]{2,1,0:T(8,128)(2,1)S(1)}, bf16[2,144,512]{2,1,0:T(8,128)(2,1)S(1)}, u32[]{:S(2)}, u32[]{:S(2)}) %collective-permute-start.2) | collective-permute-done | bytes 294944 | tf_op jit(solution)/shard_map/ppermute | solution.py:37
  17.4 4.5 %collective-permute-start.7 = (bf16[2,144,512]{2,1,0:T(8,128)(2,1)S(1)}, bf16[2,144,512]{2,1,0:T(8,128)(2,1)S(1)}, u32[]{:S(2)}, u32[]{:S(2)}) collective-permute-start(bf16[2,144,512]{2,1,0:T(8,128)(2,1)S(1)} %collective-permute-done.2), channel_id=1, source_target_pairs={{0,16},{1,113},{16,32},{17,1},{32,48},{33,17},{48,64},{49,33},{64,... | collective-permute-start | bytes 884744 | tf_op jit(solution)/shard_map/ppermute | solution.py:37
  21.9 0.7 collective-permute-start.8
  22.6 0.0 collective-permute-done.1
  22.7 0.5 collective-permute-start.3
  23.2 0.0 collective-permute-done.4.v1
  23.2 2.5 %collective-permute-start.11 = (bf16[4,128,512]{2,1,0:T(8,128)(2,1)S(1)}, bf16[4,128,512]{2,1,0:T(8,128)(2,1)S(1)}, u32[]{:S(2)}, u32[]{:S(2)}) collective-permute-start(bf16[4,128,512]{2,1,0:T(8,128)(2,1)S(1)} %collective-permute-done.4.v1), channel_id=1, source_target_pairs={{0,128},{1,131},{128,2},{129,1},{2,130},{3,129},{130,0},{131,3},{4... | collective-permute-start | bytes 1572872 | tf_op jit(solution)/shard_map/ppermute | solution.py:37
  25.7 0.8 collective-permute-done.7
  26.4 2.4 %collective-permute-done.8 = bf16[1,144,512]{2,1,0:T(8,128)(2,1)S(1)} collective-permute-done((bf16[1,144,512]{2,1,0:T(8,128)(2,1)S(1)}, bf16[1,144,512]{2,1,0:T(8,128)(2,1)S(1)}, u32[]{:S(2)}, u32[]{:S(2)}) %collective-permute-start.8) | collective-permute-done | bytes 147488 | tf_op jit(solution)/shard_map/ppermute | solution.py:37
  28.8 2.1 %collective-permute-start.9 = (bf16[3,144,512]{2,1,0:T(8,128)(2,1)S(1)}, bf16[3,144,512]{2,1,0:T(8,128)(2,1)S(1)}, u32[]{:S(2)}, u32[]{:S(2)}) collective-permute-start(bf16[3,144,512]{2,1,0:T(8,128)(2,1)S(1)} %constant_dynamic-update-slice_fusion.4.rest), channel_id=1, source_target_pairs={{0,1},{1,0},{2,3},{3,2},{4,5},{5,4},{6,7},{7,6},{8,9},{9,8},{10,11... | collective-permute-start | bytes 1327112 | tf_op jit(solution)/shard_map/ppermute | solution.py:41
  31.0 0.1 collective-permute-start.6
  31.1 2.8 %collective-permute-start.5 = (bf16[2,128,512]{2,1,0:T(8,128)(2,1)S(1)}, bf16[2,128,512]{2,1,0:T(8,128)(2,1)S(1)}, u32[]{:S(2)}, u32[]{:S(2)}) collective-permute-start(bf16[2,128,512]{2,1,0:T(8,128)(2,1)S(1)} %get-tuple-element.59), channel_id=1, source_target_pairs={{0,4},{1,13},{4,8},{5,1},{8,12},{9,5},{12,0},{13,9},{2,6},{3,15},{... | collective-permute-start | bytes 786440 | tf_op jit(solution)/shard_map/ppermute | solution.py:37
  33.9 0.0 collective-permute-done.6.v3
  33.9 2.6 %collective-permute-start.10 = (bf16[2,128,512]{2,1,0:T(8,128)(2,1)S(1)}, bf16[2,128,512]{2,1,0:T(8,128)(2,1)S(1)}, u32[]{:S(2)}, u32[]{:S(2)}) collective-permute-start(bf16[2,128,512]{2,1,0:T(8,128)(2,1)S(1)} %slice.18), channel_id=1, source_target_pairs={{0,128},{1,131},{128,2},{129,1},{2,130},{3,129},{130,0},{131,3},{4... | collective-permute-start | bytes 786440 | tf_op jit(solution)/shard_map/ppermute | solution.py:37
  36.5 0.7 collective-permute-done.5.v2
  37.2 2.5 %collective-permute-start.12 = (bf16[2,128,512]{2,1,0:T(8,128)(2,1)S(1)}, bf16[2,128,512]{2,1,0:T(8,128)(2,1)S(1)}, u32[]{:S(2)}, u32[]{:S(2)}) collective-permute-start(bf16[2,128,512]{2,1,0:T(8,128)(2,1)S(1)} %collective-permute-done.5.v2), channel_id=1, source_target_pairs={{0,128},{1,131},{128,2},{129,1},{2,130},{3,129},{130,0},{131,3},{4... | collective-permute-start | bytes 786440 | tf_op jit(solution)/shard_map/ppermute | solution.py:37
  39.7 0.0 collective-permute-done.3.w1
  39.7 3.0 %shard_map.51 = (bf16[1280,1024]{1,0:T(8,128)(2,1)S(1)}, bf16[5,512,256]{2,1,0:T(8,128)(2,1)S(1)}, bf16[1024,512]{1,0:T(8,128)(2,1)S(1)}, bf16[640,1024]{1,0:T(8,128)(2,1)}, bf16[1024,512]{1,0:T(8,128)(2,1)}) custom-call(bf16[2,144,512]{2,1,0:T(8,128)(2,1)S(1)} %constant_dynamic-update-slice_fusion.chip, ...), custom_call_target="tpu_custom_call" | custom-call | flops 1342177280 | bytes 2097152 | tf_op jit(solution)/shard_map/pallas_call | solution.py:309
  42.7 0.0 collective-permute-done.11.v1
  42.8 1.2 %collective-permute-start.13 = (bf16[2,128,512]{2,1,0:T(8,128)(2,1)S(1)}, bf16[2,128,512]{2,1,0:T(8,128)(2,1)S(1)}, u32[]{:S(2)}, u32[]{:S(2)}) collective-permute-start(bf16[2,128,512]{2,1,0:T(8,128)(2,1)S(1)} %slice.23), channel_id=1, source_target_pairs={{0,1},{1,0},{2,3},{3,2},{4,5},{5,4},{6,7},{7,6},{8,9},{9,8},{10,11... | collective-permute-start | bytes 786440 | tf_op jit(solution)/shard_map/ppermute | solution.py:41
  44.0 0.0 collective-permute-done.9.w2
  44.0 3.2 %shard_map.52 = (bf16[768,1024]{1,0:T(8,128)(2,1)S(1)}, bf16[3,512,256]{2,1,0:T(8,128)(2,1)S(1)}, bf16[8,256,256]{2,1,0:T(8,128)(2,1)S(1)}, bf16[384,1024]{1,0:T(8,128)(2,1)}) custom-call(bf16[3,144,512]{2,1,0:T(8,128)(2,1)S(1)} %constant_dynamic-update-slice_fusion.4.rest, bf16[3,144,512]{2,1,0:T(8,128)(2,1)S(1)} %collective-permute-done.9.w2, ...), custom_call_target="tpu_custom_call" | custom-call | flops 4294967296 | bytes 2097152 | tf_op jit(solution)/shard_map/pallas_call | solution.py:325
  47.2 0.0 collective-permute-done.10.v0
  47.2 0.0 collective-permute-done.12.v2
  47.2 0.0 collective-permute-done.13.v3
  47.2 2.6 %shard_map.53 = (bf16[1280,1024]{1,0:T(8,128)(2,1)S(1)}, bf16[1024,512]{1,0:T(8,128)(2,1)S(1)}, bf16[640,1024]{1,0:T(8,128)(2,1)}, bf16[1024,512]{1,0:T(8,128)(2,1)}) custom-call(bf16[2,144,512]{2,1,0:T(8,128)(2,1)S(1)} %constant_dynamic-update-slice_fusion.chip, bf16[4,144,512]{2,1,0:T(8,128)(2,1)S(1)} %constant_dynamic-update-slice_fusion.2.near, ...), custom_call_target="tpu_custom_call" | custom-call | flops 1342177280 | bytes 2097152 | tf_op jit(solution)/shard_map/pallas_call | solution.py:340
  49.9 4.0 %shard_map.54 = (bf16[768,1024]{1,0:T(8,128)(2,1)S(1)}, bf16[1024,512]{1,0:T(8,128)(2,1)}, bf16[384,1024]{1,0:T(8,128)(2,1)}) custom-call(bf16[3,144,512]{2,1,0:T(8,128)(2,1)S(1)} %constant_dynamic-update-slice_fusion.4.rest, bf16[3,144,512]{2,1,0:T(8,128)(2,1)S(1)} %collective-permute-done.9.w2, bf16[1280,1024]{1,0:T(8,128)(2,1)S(1)} %get-tuple-element.33.exch0, ...), custom_call_target="tpu_custom_call" | custom-call | flops 4294967296 | bytes 2097152 | tf_op jit(solution)/shard_map/pallas_call | solution.py:355
  53.9 3.8 %shard_map.56 = bf16[16,256,256]{2,1,0:T(8,128)(2,1)} custom-call(s32[4]{0:T(128)S(1)} %pad_add_fusion.position, bf16[5,512,256]{2,1,0:T(8,128)(2,1)S(1)} %get-tuple-element.34.scaled0, bf16[3,512,256]{2,1,0:T(8,128)(2,1)S(1)} %get-tuple-element.53.scaled1, bf16[1280,1024]{1,0:T(8,128)(2,1)S(1)} %get-tuple-element.40.exch2.exch0, ...), custom_call_target="tpu_custom_call" | custom-call | flops 2147483648 | bytes 2097152 | tf_op jit(solution)/shard_map/pallas_call | solution.py:370
  57.6 0.0 copy-start.1
  57.6 5.4 %all-to-all-start = ((bf16[16,256,256]{2,1,0:T(8,128)(2,1)}), bf16[16,256,256]{2,1,0:T(8,128)(2,1)S(1)}, u32[]{:S(2)}, u32[]{:S(2)}) async-start(bf16[16,256,256]{2,1,0:T(8,128)(2,1)} %shard_map.56), calls=%async_computation | async-start | bytes 4194304 | tf_op jit(solution)/shard_map/all_to_all | solution.py:380
  63.1 0.0 copy-done.1
  63.1 0.4 collective-permute-start.14
  63.5 2.4 %collective-permute-done.14.returned = bf16[1024,512]{1,0:T(8,128)(2,1)S(1)} collective-permute-done((bf16[1024,512]{1,0:T(8,128)(2,1)S(1)}, bf16[1024,512]{1,0:T(8,128)(2,1)S(1)}, u32[]{:S(2)}, u32[]{:S(2)}) %collective-permute-start.14) | collective-permute-done | bytes 1048608 | tf_op jit(solution)/shard_map/ppermute | solution.py:41
  65.8 5.8 %shard_map.55 = (bf16[128,512]{1,0:T(8,128)(2,1)}, bf16[128,512]{1,0:T(8,128)(2,1)}, bf16[128,512]{1,0:T(8,128)(2,1)}, bf16[128,512]{1,0:T(8,128)(2,1)}, bf16[12...) custom-call(bf16[640,1024]{1,0:T(8,128)(2,1)} %get-tuple-element.32.early0, ...), custom_call_target="tpu_custom_call" | custom-call | flops 2147483648 | bytes 2097152 | tf_op jit(solution)/shard_map/pallas_call | solution.py:381
  71.6 0.0 copy-start
  71.6 3.9 %collective-permute-start.15 = (bf16[128,512]{1,0:T(8,128)(2,1)}, bf16[128,512]{1,0:T(8,128)(2,1)S(1)}, u32[]{:S(2)}, u32[]{:S(2)}) collective-permute-start(bf16[128,512]{1,0:T(8,128)(2,1)} %get-tuple-element.45), channel_id=1, source_target_pairs={{0,64},{1,65},{16,80},{17,81},{32,96},{33,97},{48,112},{49,113},{6... | collective-permute-start | bytes 393224 | tf_op jit(solution)/shard_map/ppermute | solution.py:37
  75.5 1.3 %collective-permute-start.16 = (bf16[128,512]{1,0:T(8,128)(2,1)}, bf16[128,512]{1,0:T(8,128)(2,1)S(1)}, u32[]{:S(2)}, u32[]{:S(2)}) collective-permute-start(bf16[128,512]{1,0:T(8,128)(2,1)} %get-tuple-element.46), channel_id=1, source_target_pairs={{0,80},{1,49},{16,96},{17,65},{32,112},{33,81},{48,0},{49,97},{64,... | collective-permute-start | bytes 393224 | tf_op jit(solution)/shard_map/ppermute | solution.py:37
  76.8 3.2 %collective-permute-start.17 = (bf16[128,512]{1,0:T(8,128)(2,1)}, bf16[128,512]{1,0:T(8,128)(2,1)S(1)}, u32[]{:S(2)}, u32[]{:S(2)}) collective-permute-start(bf16[128,512]{1,0:T(8,128)(2,1)} %get-tuple-element.47), channel_id=1, source_target_pairs={{0,48},{1,81},{16,64},{17,97},{32,80},{33,113},{48,96},{49,1},{64,... | collective-permute-start | bytes 393224 | tf_op jit(solution)/shard_map/ppermute | solution.py:37
  80.0 0.0 collective-permute-start.18
  80.0 3.6 %collective-permute-start.19 = (bf16[128,512]{1,0:T(8,128)(2,1)}, bf16[128,512]{1,0:T(8,128)(2,1)S(1)}, u32[]{:S(2)}, u32[]{:S(2)}) collective-permute-start(bf16[128,512]{1,0:T(8,128)(2,1)} %get-tuple-element.49), channel_id=1, source_target_pairs={{0,32},{1,97},{16,48},{17,113},{32,64},{33,1},{48,80},{49,17},{64,... | collective-permute-start | bytes 393224 | tf_op jit(solution)/shard_map/ppermute | solution.py:37
  83.6 0.6 collective-permute-done.15
  84.1 2.1 %collective-permute-start.20 = (bf16[128,512]{1,0:T(8,128)(2,1)}, bf16[128,512]{1,0:T(8,128)(2,1)S(1)}, u32[]{:S(2)}, u32[]{:S(2)}) collective-permute-start(bf16[128,512]{1,0:T(8,128)(2,1)} %get-tuple-element.50), channel_id=1, source_target_pairs={{0,112},{1,17},{16,0},{17,33},{32,16},{33,49},{48,32},{49,65},{64,... | collective-permute-start | bytes 393224 | tf_op jit(solution)/shard_map/ppermute | solution.py:37
  86.3 0.4 collective-permute-done.16
  86.7 3.3 %collective-permute-start.21 = (bf16[128,512]{1,0:T(8,128)(2,1)}, bf16[128,512]{1,0:T(8,128)(2,1)S(1)}, u32[]{:S(2)}, u32[]{:S(2)}) collective-permute-start(bf16[128,512]{1,0:T(8,128)(2,1)} %get-tuple-element.51), channel_id=1, source_target_pairs={{0,16},{1,113},{16,32},{17,1},{32,48},{33,17},{48,64},{49,33},{64,... | collective-permute-start | bytes 393224 | tf_op jit(solution)/shard_map/ppermute | solution.py:37
  90.0 7.3 %all-to-all-done.parts = bf16[16,256,256]{2,1,0:T(8,128)(2,1)S(1)} async-done(((bf16[16,256,256]{2,1,0:T(8,128)(2,1)}), bf16[16,256,256]{2,1,0:T(8,128)(2,1)S(1)}, u32[]{:S(2)}, u32[]{:S(2)}) %all-to-all-start) | async-done | bytes 2097184 | tf_op jit(solution)/shard_map/all_to_all | solution.py:380
  97.2 0.8 shard_map.57
  98.1 0.0 collective-permute-done.17
  98.1 1.3 %collective-permute-start.22 = (f32[128,256]{1,0:T(8,128)S(1)}, f32[128,256]{1,0:T(8,128)S(1)}, u32[]{:S(2)}, u32[]{:S(2)}) collective-permute-start(f32[128,256]{1,0:T(8,128)S(1)} %get-tuple-element.57), channel_id=1, source_target_pairs={{0,1},{1,0},{2,3},{3,2},{4,5},{5,4},{6,7},{7,6},{8,9},{9,8},{10,11... | collective-permute-start | bytes 393224 | tf_op jit(solution)/shard_map/ppermute | solution.py:41
  99.4 0.0 collective-permute-done.18
  99.4 0.0 collective-permute-done.19
  99.4 0.0 collective-permute-done.20
  99.4 0.8 collective-permute-done.21
  100.2 0.0 copy-done
  100.2 0.8 multiply_bitcast_fusion
  101.1 0.0 collective-permute-done.22.received
  101.1 1.4 %shard_map.58 = f32[4,128,128]{2,1,0:T(8,128)} custom-call(s32[4]{0:T(128)S(1)} %pad_add_fusion.position, f32[128,256]{1,0:T(8,128)S(1)} %get-tuple-element.56.keep, f32[128,256]{1,0:T(8,128)S(1)} %collective-permute-done.22.received), custom_call_target="tpu_custom_call" | custom-call | bytes 2097152 | tf_op jit(solution)/shard_map/pallas_call | solution.py:404
  (10 shorter events, 0.2 us)
Async XLA Ops:
  3.1 4.3 %collective-permute-start = (bf16[1,144,512]{2,1,0:T(8,128)(2,1)S(1)}, bf16[1,144,512]{2,1,0:T(8,128)(2,1)S(1)}, u32[]{:S(2)}, u32[]{:S(2)}) collective-permute-start(bf16[1,144,512]{2,1,0:T(8,128)(2,1)S(1)} %get-tuple-element.30), channel_id=1, source_target_pairs={{0,1},{1,0},{2,3},{3,2},{4,5},{5,4},{6,7},{7,6},{8,9},{9,8},{10,11... | collective-permute-start | bytes 442376 | tf_op jit(solution)/shard_map/ppermute | solution.py:41
  7.4 10.0 %collective-permute-start.2 = (bf16[2,144,512]{2,1,0:T(8,128)(2,1)S(1)}, bf16[2,144,512]{2,1,0:T(8,128)(2,1)S(1)}, u32[]{:S(2)}, u32[]{:S(2)}) collective-permute-start(bf16[2,144,512]{2,1,0:T(8,128)(2,1)S(1)} %constant_dynamic-update-slice_fusion.chip), channel_id=1, source_target_pairs={{0,32},{1,97},{16,48},{17,113},{32,64},{33,1},{48,80},{49,17},{64,... | collective-permute-start | bytes 884744 | tf_op jit(solution)/shard_map/ppermute | solution.py:37
  11.8 10.8 %collective-permute-start.1 = (bf16[2,144,512]{2,1,0:T(8,128)(2,1)S(1)}, bf16[2,144,512]{2,1,0:T(8,128)(2,1)S(1)}, u32[]{:S(2)}, u32[]{:S(2)}) collective-permute-start(bf16[2,144,512]{2,1,0:T(8,128)(2,1)S(1)} %constant_dynamic-update-slice_fusion.chip), channel_id=1, source_target_pairs={{0,16},{1,113},{16,32},{17,1},{32,48},{33,17},{48,64},{49,33},{64,... | collective-permute-start | bytes 884744 | tf_op jit(solution)/shard_map/ppermute | solution.py:37
  12.5 10.6 %collective-permute-start.4 = (bf16[4,128,512]{2,1,0:T(8,128)(2,1)S(1)}, bf16[4,128,512]{2,1,0:T(8,128)(2,1)S(1)}, u32[]{:S(2)}, u32[]{:S(2)}) collective-permute-start(bf16[4,128,512]{2,1,0:T(8,128)(2,1)S(1)} %get-tuple-element.31.v0), channel_id=1, source_target_pairs={{0,4},{1,13},{4,8},{5,1},{8,12},{9,5},{12,0},{13,9},{2,6},{3,15},{... | collective-permute-start | bytes 1572872 | tf_op jit(solution)/shard_map/ppermute | solution.py:37
  17.4 9.0 %collective-permute-start.7 = (bf16[2,144,512]{2,1,0:T(8,128)(2,1)S(1)}, bf16[2,144,512]{2,1,0:T(8,128)(2,1)S(1)}, u32[]{:S(2)}, u32[]{:S(2)}) collective-permute-start(bf16[2,144,512]{2,1,0:T(8,128)(2,1)S(1)} %collective-permute-done.2), channel_id=1, source_target_pairs={{0,16},{1,113},{16,32},{17,1},{32,48},{33,17},{48,64},{49,33},{64,... | collective-permute-start | bytes 884744 | tf_op jit(solution)/shard_map/ppermute | solution.py:37
  21.9 6.8 %collective-permute-start.8 = (bf16[1,144,512]{2,1,0:T(8,128)(2,1)S(1)}, bf16[1,144,512]{2,1,0:T(8,128)(2,1)S(1)}, u32[]{:S(2)}, u32[]{:S(2)}) collective-permute-start(bf16[1,144,512]{2,1,0:T(8,128)(2,1)S(1)} %slice.22), channel_id=1, source_target_pairs={{0,32},{1,97},{16,48},{17,113},{32,64},{33,1},{48,80},{49,17},{64,... | collective-permute-start | bytes 442376 | tf_op jit(solution)/shard_map/ppermute | solution.py:37
  22.7 17.0 %collective-permute-start.3 = (bf16[4,144,512]{2,1,0:T(8,128)(2,1)S(1)}, bf16[4,144,512]{2,1,0:T(8,128)(2,1)S(1)}, u32[]{:S(2)}, u32[]{:S(2)}) collective-permute-start(bf16[4,144,512]{2,1,0:T(8,128)(2,1)S(1)} %constant_dynamic-update-slice_fusion.2.near), channel_id=1, source_target_pairs={{0,1},{1,0},{2,3},{3,2},{4,5},{5,4},{6,7},{7,6},{8,9},{9,8},{10,11... | collective-permute-start | bytes 1769480 | tf_op jit(solution)/shard_map/ppermute | solution.py:41
  23.2 19.5 %collective-permute-start.11 = (bf16[4,128,512]{2,1,0:T(8,128)(2,1)S(1)}, bf16[4,128,512]{2,1,0:T(8,128)(2,1)S(1)}, u32[]{:S(2)}, u32[]{:S(2)}) collective-permute-start(bf16[4,128,512]{2,1,0:T(8,128)(2,1)S(1)} %collective-permute-done.4.v1), channel_id=1, source_target_pairs={{0,128},{1,131},{128,2},{129,1},{2,130},{3,129},{130,0},{131,3},{4... | collective-permute-start | bytes 1572872 | tf_op jit(solution)/shard_map/ppermute | solution.py:37
  28.8 15.2 %collective-permute-start.9 = (bf16[3,144,512]{2,1,0:T(8,128)(2,1)S(1)}, bf16[3,144,512]{2,1,0:T(8,128)(2,1)S(1)}, u32[]{:S(2)}, u32[]{:S(2)}) collective-permute-start(bf16[3,144,512]{2,1,0:T(8,128)(2,1)S(1)} %constant_dynamic-update-slice_fusion.4.rest), channel_id=1, source_target_pairs={{0,1},{1,0},{2,3},{3,2},{4,5},{5,4},{6,7},{7,6},{8,9},{9,8},{10,11... | collective-permute-start | bytes 1327112 | tf_op jit(solution)/shard_map/ppermute | solution.py:41
  31.0 2.9 %collective-permute-start.6 = (bf16[2,128,512]{2,1,0:T(8,128)(2,1)S(1)}, bf16[2,128,512]{2,1,0:T(8,128)(2,1)S(1)}, u32[]{:S(2)}, u32[]{:S(2)}) collective-permute-start(bf16[2,128,512]{2,1,0:T(8,128)(2,1)S(1)} %get-tuple-element.58), channel_id=1, source_target_pairs={{0,1},{1,0},{2,3},{3,2},{4,5},{5,4},{6,7},{7,6},{8,9},{9,8},{10,11... | collective-permute-start | bytes 786440 | tf_op jit(solution)/shard_map/ppermute | solution.py:41
  31.1 6.1 %collective-permute-start.5 = (bf16[2,128,512]{2,1,0:T(8,128)(2,1)S(1)}, bf16[2,128,512]{2,1,0:T(8,128)(2,1)S(1)}, u32[]{:S(2)}, u32[]{:S(2)}) collective-permute-start(bf16[2,128,512]{2,1,0:T(8,128)(2,1)S(1)} %get-tuple-element.59), channel_id=1, source_target_pairs={{0,4},{1,13},{4,8},{5,1},{8,12},{9,5},{12,0},{13,9},{2,6},{3,15},{... | collective-permute-start | bytes 786440 | tf_op jit(solution)/shard_map/ppermute | solution.py:37
  33.9 13.3 %collective-permute-start.10 = (bf16[2,128,512]{2,1,0:T(8,128)(2,1)S(1)}, bf16[2,128,512]{2,1,0:T(8,128)(2,1)S(1)}, u32[]{:S(2)}, u32[]{:S(2)}) collective-permute-start(bf16[2,128,512]{2,1,0:T(8,128)(2,1)S(1)} %slice.18), channel_id=1, source_target_pairs={{0,128},{1,131},{128,2},{129,1},{2,130},{3,129},{130,0},{131,3},{4... | collective-permute-start | bytes 786440 | tf_op jit(solution)/shard_map/ppermute | solution.py:37
  37.2 10.0 %collective-permute-start.12 = (bf16[2,128,512]{2,1,0:T(8,128)(2,1)S(1)}, bf16[2,128,512]{2,1,0:T(8,128)(2,1)S(1)}, u32[]{:S(2)}, u32[]{:S(2)}) collective-permute-start(bf16[2,128,512]{2,1,0:T(8,128)(2,1)S(1)} %collective-permute-done.5.v2), channel_id=1, source_target_pairs={{0,128},{1,131},{128,2},{129,1},{2,130},{3,129},{130,0},{131,3},{4... | collective-permute-start | bytes 786440 | tf_op jit(solution)/shard_map/ppermute | solution.py:37
  42.8 4.5 %collective-permute-start.13 = (bf16[2,128,512]{2,1,0:T(8,128)(2,1)S(1)}, bf16[2,128,512]{2,1,0:T(8,128)(2,1)S(1)}, u32[]{:S(2)}, u32[]{:S(2)}) collective-permute-start(bf16[2,128,512]{2,1,0:T(8,128)(2,1)S(1)} %slice.23), channel_id=1, source_target_pairs={{0,1},{1,0},{2,3},{3,2},{4,5},{5,4},{6,7},{7,6},{8,9},{9,8},{10,11... | collective-permute-start | bytes 786440 | tf_op jit(solution)/shard_map/ppermute | solution.py:41
  57.6 5.4 %copy-start.1 = (bf16[1024,512]{1,0:T(8,128)(2,1)S(1)}, bf16[1024,512]{1,0:T(8,128)(2,1)}, u32[]{:S(2)}) copy-start(bf16[1024,512]{1,0:T(8,128)(2,1)} %get-tuple-element.44) | copy-start | bytes 3145732
  57.6 39.6 %all-to-all-start = ((bf16[16,256,256]{2,1,0:T(8,128)(2,1)}), bf16[16,256,256]{2,1,0:T(8,128)(2,1)S(1)}, u32[]{:S(2)}, u32[]{:S(2)}) async-start(bf16[16,256,256]{2,1,0:T(8,128)(2,1)} %shard_map.56), calls=%async_computation | async-start | bytes 4194304 | tf_op jit(solution)/shard_map/all_to_all | solution.py:380
  63.1 2.7 %collective-permute-start.14 = (bf16[1024,512]{1,0:T(8,128)(2,1)S(1)}, bf16[1024,512]{1,0:T(8,128)(2,1)S(1)}, u32[]{:S(2)}, u32[]{:S(2)}) collective-permute-start(bf16[1024,512]{1,0:T(8,128)(2,1)S(1)} %copy-done.1), channel_id=1, source_target_pairs={{0,1},{1,0},{2,3},{3,2},{4,5},{5,4},{6,7},{7,6},{8,9},{9,8},{10,11... | collective-permute-start | bytes 3145736 | tf_op jit(solution)/shard_map/ppermute | solution.py:41
  71.6 28.6 %copy-start = (bf16[128,512]{1,0:T(8,128)(2,1)S(1)}, bf16[128,512]{1,0:T(8,128)(2,1)}, u32[]{:S(2)}) copy-start(bf16[128,512]{1,0:T(8,128)(2,1)} %get-tuple-element.52) | copy-start | bytes 393220
  71.6 12.5 %collective-permute-start.15 = (bf16[128,512]{1,0:T(8,128)(2,1)}, bf16[128,512]{1,0:T(8,128)(2,1)S(1)}, u32[]{:S(2)}, u32[]{:S(2)}) collective-permute-start(bf16[128,512]{1,0:T(8,128)(2,1)} %get-tuple-element.45), channel_id=1, source_target_pairs={{0,64},{1,65},{16,80},{17,81},{32,96},{33,97},{48,112},{49,113},{6... | collective-permute-start | bytes 393224 | tf_op jit(solution)/shard_map/ppermute | solution.py:37
  75.5 11.2 %collective-permute-start.16 = (bf16[128,512]{1,0:T(8,128)(2,1)}, bf16[128,512]{1,0:T(8,128)(2,1)S(1)}, u32[]{:S(2)}, u32[]{:S(2)}) collective-permute-start(bf16[128,512]{1,0:T(8,128)(2,1)} %get-tuple-element.46), channel_id=1, source_target_pairs={{0,80},{1,49},{16,96},{17,65},{32,112},{33,81},{48,0},{49,97},{64,... | collective-permute-start | bytes 393224 | tf_op jit(solution)/shard_map/ppermute | solution.py:37
  76.8 21.2 %collective-permute-start.17 = (bf16[128,512]{1,0:T(8,128)(2,1)}, bf16[128,512]{1,0:T(8,128)(2,1)S(1)}, u32[]{:S(2)}, u32[]{:S(2)}) collective-permute-start(bf16[128,512]{1,0:T(8,128)(2,1)} %get-tuple-element.47), channel_id=1, source_target_pairs={{0,48},{1,81},{16,64},{17,97},{32,80},{33,113},{48,96},{49,1},{64,... | collective-permute-start | bytes 393224 | tf_op jit(solution)/shard_map/ppermute | solution.py:37
  80.0 19.4 %collective-permute-start.18 = (bf16[128,512]{1,0:T(8,128)(2,1)}, bf16[128,512]{1,0:T(8,128)(2,1)S(1)}, u32[]{:S(2)}, u32[]{:S(2)}) collective-permute-start(bf16[128,512]{1,0:T(8,128)(2,1)} %get-tuple-element.48), channel_id=1, source_target_pairs={{0,96},{1,33},{16,112},{17,49},{32,0},{33,65},{48,16},{49,81},{64,... | collective-permute-start | bytes 393224 | tf_op jit(solution)/shard_map/ppermute | solution.py:37
  80.0 19.4 %collective-permute-start.19 = (bf16[128,512]{1,0:T(8,128)(2,1)}, bf16[128,512]{1,0:T(8,128)(2,1)S(1)}, u32[]{:S(2)}, u32[]{:S(2)}) collective-permute-start(bf16[128,512]{1,0:T(8,128)(2,1)} %get-tuple-element.49), channel_id=1, source_target_pairs={{0,32},{1,97},{16,48},{17,113},{32,64},{33,1},{48,80},{49,17},{64,... | collective-permute-start | bytes 393224 | tf_op jit(solution)/shard_map/ppermute | solution.py:37
  84.1 15.3 %collective-permute-start.20 = (bf16[128,512]{1,0:T(8,128)(2,1)}, bf16[128,512]{1,0:T(8,128)(2,1)S(1)}, u32[]{:S(2)}, u32[]{:S(2)}) collective-permute-start(bf16[128,512]{1,0:T(8,128)(2,1)} %get-tuple-element.50), channel_id=1, source_target_pairs={{0,112},{1,17},{16,0},{17,33},{32,16},{33,49},{48,32},{49,65},{64,... | collective-permute-start | bytes 393224 | tf_op jit(solution)/shard_map/ppermute | solution.py:37
  86.7 13.6 %collective-permute-start.21 = (bf16[128,512]{1,0:T(8,128)(2,1)}, bf16[128,512]{1,0:T(8,128)(2,1)S(1)}, u32[]{:S(2)}, u32[]{:S(2)}) collective-permute-start(bf16[128,512]{1,0:T(8,128)(2,1)} %get-tuple-element.51), channel_id=1, source_target_pairs={{0,16},{1,113},{16,32},{17,1},{32,48},{33,17},{48,64},{49,33},{64,... | collective-permute-start | bytes 393224 | tf_op jit(solution)/shard_map/ppermute | solution.py:37
  98.1 3.0 %collective-permute-start.22 = (f32[128,256]{1,0:T(8,128)S(1)}, f32[128,256]{1,0:T(8,128)S(1)}, u32[]{:S(2)}, u32[]{:S(2)}) collective-permute-start(f32[128,256]{1,0:T(8,128)S(1)} %get-tuple-element.57), channel_id=1, source_target_pairs={{0,1},{1,0},{2,3},{3,2},{4,5},{5,4},{6,7},{7,6},{8,9},{9,8},{10,11... | collective-permute-start | bytes 393224 | tf_op jit(solution)/shard_map/ppermute | solution.py:41

commit v3 on v2

--- a/solution.py
+++ b/solution.py
@@ -252,21 +252,27 @@
 
 def total(position, parts, keep, send):
     core = position[0]
-    rows = keep.shape[0]
+    rows = keep.shape[2]
+    n = keep.shape[1]
     for out, c in ((send, 1 - core), (keep, core)):
         start = pl.multiple_of(c * rows, rows)
         acc = parts[0, pl.ds(start, rows), :].astype(F32)
         for s in range(1, parts.shape[0]):
             acc += parts[s, pl.ds(start, rows), :].astype(F32)
-        out[...] = -acc
-
-
-def place(position, keep, received, out):
+        for h in range(2):
+            out[h] = -acc[:, h * n : (h + 1) * n].T
+
+
+def place(position, keep, received, out, sems):
     core = position[0]
-    n = out.shape[1]
+    copies = []
     for h in range(2):
-        out[2 * h + core] = keep[:, h * n : (h + 1) * n].T
-        out[2 * h + 1 - core] = received[:, h * n : (h + 1) * n].T
+        copies += started(
+            pltpu.make_async_copy(keep.at[h], out.at[2 * h + core], sems.at[2 * h]),
+            pltpu.make_async_copy(received.at[h], out.at[2 * h + 1 - core], sems.at[2 * h + 1]),
+        )
+    for copy in copies:
+        copy.wait()
 
 
 def step(green, vectors, weight):
@@ -400,8 +406,10 @@
     minus = -weight[0]
     green_cot = (minus * cot)[None]
 
-    keep, send = call(total, (shape((m // 4, 2 * o), F32),) * 2, [SMEM, VMEM], 16)(position, grad)
-    chol_grad = call(place, shape((4, o, m // 4), F32), [SMEM, VMEM, VMEM], 16)(position, keep, swap(send))
+    keep, send = call(total, (shape((2, o, m // 4), F32),) * 2, [SMEM, VMEM], 16)(position, grad)
+    chol_grad = call(
+        place, pltpu.HBM((4, o, m // 4), F32), [SMEM, VMEM, VMEM], 16, scratch=[dma((4,))], out_specs=HBM
+    )(position, keep, swap(send))
     return green_cot, chol_grad
 
 

time: 103 us -> 103 us (level)
  transfers between devices with their start and end apart: 24 -> 24, of which waited for: 10 -> 10; matrix products, arithmetic and copies ran while one was open for 1% -> 1% of each run, Pallas kernels for 12% -> 13%
where the time goes in v3:
time: 103 us
  starting transfers between devices  55.1 us (53%)
  Pallas kernels  26.3 us (26%)
  waiting for transfers between devices  18.4 us (18%)
  between operations  1.67 us (2%)
    ppermute x16, starting transfers between devices, opposed(): return lax.ppermute(block, names, route)  40.7 us
    ppermute x7, starting transfers between devices, swap(): return lax.ppermute(block, 'core', [(0, 1), (1, 0)])  8.93 us
    ppermute x16, waiting for transfers between devices, opposed(): return lax.ppermute(block, names, route)  7.74 us
    all_to_all x1, waiting for transfers between devices, step(): grad = lax.all_to_all(grad, PLANE, 0, 0, tiled=True)  7.28 us
    pallas_call x1, Pallas kernels, step(): call(finish, tuple((pltpu.HBM((o, m), BF16) for _ in range(zs))), [HBM] *...  5.76 us
    all_to_all x1, starting transfers between devices, step(): grad = lax.all_to_all(grad, PLANE, 0, 0, tiled=True)  5.42 us
    pallas_call x1, Pallas kernels, step(): call(second, (pltpu.VMEM((2 * nl * o, half * o), BF16), pltpu.HBM((zs * o...  3.99 us
    pallas_call x1, Pallas kernels, step(): call(gradient, pltpu.HBM((plane, m // 2, 2 * o), BF16), [SMEM] + [VMEM] *...  3.76 us
  transfers between devices with their start and end apart: 24, of which 10 were waited for; matrix products, arithmetic and copies ran while one was open for 1% of the time, Pallas kernels for 13%

profile of v3, /device:TPU:1, one launch (start us, length us, event | category | flops | bytes accessed | tf_op | source)
XLA Modules:
  0.0 102.5 jit_solution(11082105766650143871)
XLA Ops:
  1.3 0.1 pad_add_fusion.position
  1.4 1.7 %shard_map.50 = (bf16[1,144,512]{2,1,0:T(8,128)(2,1)S(1)}, bf16[4,128,512]{2,1,0:T(8,128)(2,1)S(1)}) custom-call(s32[4]{0:T(128)S(1)} %pad_add_fusion.position, f32[1]{0:T(128)S(6)} %copy.8.weight, bf16[1,128,512]{2,1,0:T(8,128)(2,1)} %green.1, bf16[4,128,512]{2,1,0:T(8,128)(2,1)} %vectors.1), custom_call_target="tpu_custom_call" | custom-call | bytes 2097152 | tf_op jit(solution)/shard_map/pallas_call | solution.py:287
  3.1 3.3 %collective-permute-start = (bf16[1,144,512]{2,1,0:T(8,128)(2,1)S(1)}, bf16[1,144,512]{2,1,0:T(8,128)(2,1)S(1)}, u32[]{:S(2)}, u32[]{:S(2)}) collective-permute-start(bf16[1,144,512]{2,1,0:T(8,128)(2,1)S(1)} %get-tuple-element.30), channel_id=1, source_target_pairs={{0,1},{1,0},{2,3},{3,2},{4,5},{5,4},{6,7},{7,6},{8,9},{9,8},{10,11... | collective-permute-start | bytes 442376 | tf_op jit(solution)/shard_map/ppermute | solution.py:41
  6.4 1.0 collective-permute-done
  7.4 4.4 %collective-permute-start.2 = (bf16[2,144,512]{2,1,0:T(8,128)(2,1)S(1)}, bf16[2,144,512]{2,1,0:T(8,128)(2,1)S(1)}, u32[]{:S(2)}, u32[]{:S(2)}) collective-permute-start(bf16[2,144,512]{2,1,0:T(8,128)(2,1)S(1)} %constant_dynamic-update-slice_fusion.chip), channel_id=1, source_target_pairs={{0,32},{1,97},{16,48},{17,113},{32,64},{33,1},{48,80},{49,17},{64,... | collective-permute-start | bytes 884744 | tf_op jit(solution)/shard_map/ppermute | solution.py:37
  11.8 0.7 collective-permute-start.1
  12.5 2.7 %collective-permute-start.4 = (bf16[4,128,512]{2,1,0:T(8,128)(2,1)S(1)}, bf16[4,128,512]{2,1,0:T(8,128)(2,1)S(1)}, u32[]{:S(2)}, u32[]{:S(2)}) collective-permute-start(bf16[4,128,512]{2,1,0:T(8,128)(2,1)S(1)} %get-tuple-element.31.v0), channel_id=1, source_target_pairs={{0,4},{1,13},{4,8},{5,1},{8,12},{9,5},{12,0},{13,9},{2,6},{3,15},{... | collective-permute-start | bytes 1572872 | tf_op jit(solution)/shard_map/ppermute | solution.py:37
  15.3 2.2 %collective-permute-done.2 = bf16[2,144,512]{2,1,0:T(8,128)(2,1)S(1)} collective-permute-done((bf16[2,144,512]{2,1,0:T(8,128)(2,1)S(1)}, bf16[2,144,512]{2,1,0:T(8,128)(2,1)S(1)}, u32[]{:S(2)}, u32[]{:S(2)}) %collective-permute-start.2) | collective-permute-done | bytes 294944 | tf_op jit(solution)/shard_map/ppermute | solution.py:37
  17.4 4.5 %collective-permute-start.7 = (bf16[2,144,512]{2,1,0:T(8,128)(2,1)S(1)}, bf16[2,144,512]{2,1,0:T(8,128)(2,1)S(1)}, u32[]{:S(2)}, u32[]{:S(2)}) collective-permute-start(bf16[2,144,512]{2,1,0:T(8,128)(2,1)S(1)} %collective-permute-done.2), channel_id=1, source_target_pairs={{0,16},{1,113},{16,32},{17,1},{32,48},{33,17},{48,64},{49,33},{64,... | collective-permute-start | bytes 884744 | tf_op jit(solution)/shard_map/ppermute | solution.py:37
  21.9 0.7 collective-permute-start.8
  22.6 0.0 collective-permute-done.1
  22.7 0.5 collective-permute-start.3
  23.2 0.0 collective-permute-done.4.v1
  23.2 2.5 %collective-permute-start.11 = (bf16[4,128,512]{2,1,0:T(8,128)(2,1)S(1)}, bf16[4,128,512]{2,1,0:T(8,128)(2,1)S(1)}, u32[]{:S(2)}, u32[]{:S(2)}) collective-permute-start(bf16[4,128,512]{2,1,0:T(8,128)(2,1)S(1)} %collective-permute-done.4.v1), channel_id=1, source_target_pairs={{0,128},{1,131},{128,2},{129,1},{2,130},{3,129},{130,0},{131,3},{4... | collective-permute-start | bytes 1572872 | tf_op jit(solution)/shard_map/ppermute | solution.py:37
  25.7 0.8 collective-permute-done.7
  26.4 2.4 %collective-permute-done.8 = bf16[1,144,512]{2,1,0:T(8,128)(2,1)S(1)} collective-permute-done((bf16[1,144,512]{2,1,0:T(8,128)(2,1)S(1)}, bf16[1,144,512]{2,1,0:T(8,128)(2,1)S(1)}, u32[]{:S(2)}, u32[]{:S(2)}) %collective-permute-start.8) | collective-permute-done | bytes 147488 | tf_op jit(solution)/shard_map/ppermute | solution.py:37
  28.8 2.1 %collective-permute-start.9 = (bf16[3,144,512]{2,1,0:T(8,128)(2,1)S(1)}, bf16[3,144,512]{2,1,0:T(8,128)(2,1)S(1)}, u32[]{:S(2)}, u32[]{:S(2)}) collective-permute-start(bf16[3,144,512]{2,1,0:T(8,128)(2,1)S(1)} %constant_dynamic-update-slice_fusion.4.rest), channel_id=1, source_target_pairs={{0,1},{1,0},{2,3},{3,2},{4,5},{5,4},{6,7},{7,6},{8,9},{9,8},{10,11... | collective-permute-start | bytes 1327112 | tf_op jit(solution)/shard_map/ppermute | solution.py:41
  31.0 0.1 collective-permute-start.6
  31.1 2.8 %collective-permute-start.5 = (bf16[2,128,512]{2,1,0:T(8,128)(2,1)S(1)}, bf16[2,128,512]{2,1,0:T(8,128)(2,1)S(1)}, u32[]{:S(2)}, u32[]{:S(2)}) collective-permute-start(bf16[2,128,512]{2,1,0:T(8,128)(2,1)S(1)} %get-tuple-element.59), channel_id=1, source_target_pairs={{0,4},{1,13},{4,8},{5,1},{8,12},{9,5},{12,0},{13,9},{2,6},{3,15},{... | collective-permute-start | bytes 786440 | tf_op jit(solution)/shard_map/ppermute | solution.py:37
  33.9 0.0 collective-permute-done.6.v3
  33.9 2.6 %collective-permute-start.10 = (bf16[2,128,512]{2,1,0:T(8,128)(2,1)S(1)}, bf16[2,128,512]{2,1,0:T(8,128)(2,1)S(1)}, u32[]{:S(2)}, u32[]{:S(2)}) collective-permute-start(bf16[2,128,512]{2,1,0:T(8,128)(2,1)S(1)} %slice.18), channel_id=1, source_target_pairs={{0,128},{1,131},{128,2},{129,1},{2,130},{3,129},{130,0},{131,3},{4... | collective-permute-start | bytes 786440 | tf_op jit(solution)/shard_map/ppermute | solution.py:37
  36.5 0.7 collective-permute-done.5.v2
  37.2 2.5 %collective-permute-start.12 = (bf16[2,128,512]{2,1,0:T(8,128)(2,1)S(1)}, bf16[2,128,512]{2,1,0:T(8,128)(2,1)S(1)}, u32[]{:S(2)}, u32[]{:S(2)}) collective-permute-start(bf16[2,128,512]{2,1,0:T(8,128)(2,1)S(1)} %collective-permute-done.5.v2), channel_id=1, source_target_pairs={{0,128},{1,131},{128,2},{129,1},{2,130},{3,129},{130,0},{131,3},{4... | collective-permute-start | bytes 786440 | tf_op jit(solution)/shard_map/ppermute | solution.py:37
  39.7 0.0 collective-permute-done.3.w1
  39.7 3.0 %shard_map.51 = (bf16[1280,1024]{1,0:T(8,128)(2,1)S(1)}, bf16[5,512,256]{2,1,0:T(8,128)(2,1)S(1)}, bf16[1024,512]{1,0:T(8,128)(2,1)S(1)}, bf16[640,1024]{1,0:T(8,128)(2,1)}, bf16[1024,512]{1,0:T(8,128)(2,1)}) custom-call(bf16[2,144,512]{2,1,0:T(8,128)(2,1)S(1)} %constant_dynamic-update-slice_fusion.chip, ...), custom_call_target="tpu_custom_call" | custom-call | flops 1342177280 | bytes 2097152 | tf_op jit(solution)/shard_map/pallas_call | solution.py:315
  42.7 0.0 collective-permute-done.11.v1
  42.8 1.2 %collective-permute-start.13 = (bf16[2,128,512]{2,1,0:T(8,128)(2,1)S(1)}, bf16[2,128,512]{2,1,0:T(8,128)(2,1)S(1)}, u32[]{:S(2)}, u32[]{:S(2)}) collective-permute-start(bf16[2,128,512]{2,1,0:T(8,128)(2,1)S(1)} %slice.23), channel_id=1, source_target_pairs={{0,1},{1,0},{2,3},{3,2},{4,5},{5,4},{6,7},{7,6},{8,9},{9,8},{10,11... | collective-permute-start | bytes 786440 | tf_op jit(solution)/shard_map/ppermute | solution.py:41
  44.0 0.0 collective-permute-done.9.w2
  44.0 3.2 %shard_map.52 = (bf16[768,1024]{1,0:T(8,128)(2,1)S(1)}, bf16[3,512,256]{2,1,0:T(8,128)(2,1)S(1)}, bf16[8,256,256]{2,1,0:T(8,128)(2,1)S(1)}, bf16[384,1024]{1,0:T(8,128)(2,1)}) custom-call(bf16[3,144,512]{2,1,0:T(8,128)(2,1)S(1)} %constant_dynamic-update-slice_fusion.4.rest, bf16[3,144,512]{2,1,0:T(8,128)(2,1)S(1)} %collective-permute-done.9.w2, ...), custom_call_target="tpu_custom_call" | custom-call | flops 4294967296 | bytes 2097152 | tf_op jit(solution)/shard_map/pallas_call | solution.py:331
  47.2 0.0 collective-permute-done.10.v0
  47.2 0.0 collective-permute-done.12.v2
  47.2 0.0 collective-permute-done.13.v3
  47.2 2.6 %shard_map.53 = (bf16[1280,1024]{1,0:T(8,128)(2,1)S(1)}, bf16[1024,512]{1,0:T(8,128)(2,1)S(1)}, bf16[640,1024]{1,0:T(8,128)(2,1)}, bf16[1024,512]{1,0:T(8,128)(2,1)}) custom-call(bf16[2,144,512]{2,1,0:T(8,128)(2,1)S(1)} %constant_dynamic-update-slice_fusion.chip, bf16[4,144,512]{2,1,0:T(8,128)(2,1)S(1)} %constant_dynamic-update-slice_fusion.2.near, ...), custom_call_target="tpu_custom_call" | custom-call | flops 1342177280 | bytes 2097152 | tf_op jit(solution)/shard_map/pallas_call | solution.py:346
  49.9 4.0 %shard_map.54 = (bf16[768,1024]{1,0:T(8,128)(2,1)S(1)}, bf16[1024,512]{1,0:T(8,128)(2,1)}, bf16[384,1024]{1,0:T(8,128)(2,1)}) custom-call(bf16[3,144,512]{2,1,0:T(8,128)(2,1)S(1)} %constant_dynamic-update-slice_fusion.4.rest, bf16[3,144,512]{2,1,0:T(8,128)(2,1)S(1)} %collective-permute-done.9.w2, bf16[1280,1024]{1,0:T(8,128)(2,1)S(1)} %get-tuple-element.33.exch0, ...), custom_call_target="tpu_custom_call" | custom-call | flops 4294967296 | bytes 2097152 | tf_op jit(solution)/shard_map/pallas_call | solution.py:361
  53.9 3.8 %shard_map.56 = bf16[16,256,256]{2,1,0:T(8,128)(2,1)} custom-call(s32[4]{0:T(128)S(1)} %pad_add_fusion.position, bf16[5,512,256]{2,1,0:T(8,128)(2,1)S(1)} %get-tuple-element.34.scaled0, bf16[3,512,256]{2,1,0:T(8,128)(2,1)S(1)} %get-tuple-element.53.scaled1, bf16[1280,1024]{1,0:T(8,128)(2,1)S(1)} %get-tuple-element.40.exch2.exch0, ...), custom_call_target="tpu_custom_call" | custom-call | flops 2147483648 | bytes 2097152 | tf_op jit(solution)/shard_map/pallas_call | solution.py:376
  57.6 0.0 copy-start.1
  57.6 5.4 %all-to-all-start = ((bf16[16,256,256]{2,1,0:T(8,128)(2,1)}), bf16[16,256,256]{2,1,0:T(8,128)(2,1)S(1)}, u32[]{:S(2)}, u32[]{:S(2)}) async-start(bf16[16,256,256]{2,1,0:T(8,128)(2,1)} %shard_map.56), calls=%async_computation | async-start | bytes 4194304 | tf_op jit(solution)/shard_map/all_to_all | solution.py:386
  63.1 0.0 copy-done.1
  63.1 0.4 collective-permute-start.14
  63.5 2.4 %collective-permute-done.14.returned = bf16[1024,512]{1,0:T(8,128)(2,1)S(1)} collective-permute-done((bf16[1024,512]{1,0:T(8,128)(2,1)S(1)}, bf16[1024,512]{1,0:T(8,128)(2,1)S(1)}, u32[]{:S(2)}, u32[]{:S(2)}) %collective-permute-start.14) | collective-permute-done | bytes 1048608 | tf_op jit(solution)/shard_map/ppermute | solution.py:41
  65.8 5.8 %shard_map.55 = (bf16[128,512]{1,0:T(8,128)(2,1)}, bf16[128,512]{1,0:T(8,128)(2,1)}, bf16[128,512]{1,0:T(8,128)(2,1)}, bf16[128,512]{1,0:T(8,128)(2,1)}, bf16[12...) custom-call(bf16[640,1024]{1,0:T(8,128)(2,1)} %get-tuple-element.32.early0, ...), custom_call_target="tpu_custom_call" | custom-call | flops 2147483648 | bytes 2097152 | tf_op jit(solution)/shard_map/pallas_call | solution.py:387
  71.6 0.0 copy-start
  71.6 3.9 %collective-permute-start.15 = (bf16[128,512]{1,0:T(8,128)(2,1)}, bf16[128,512]{1,0:T(8,128)(2,1)S(1)}, u32[]{:S(2)}, u32[]{:S(2)}) collective-permute-start(bf16[128,512]{1,0:T(8,128)(2,1)} %get-tuple-element.45), channel_id=1, source_target_pairs={{0,64},{1,65},{16,80},{17,81},{32,96},{33,97},{48,112},{49,113},{6... | collective-permute-start | bytes 393224 | tf_op jit(solution)/shard_map/ppermute | solution.py:37
  75.5 1.3 %collective-permute-start.16 = (bf16[128,512]{1,0:T(8,128)(2,1)}, bf16[128,512]{1,0:T(8,128)(2,1)S(1)}, u32[]{:S(2)}, u32[]{:S(2)}) collective-permute-start(bf16[128,512]{1,0:T(8,128)(2,1)} %get-tuple-element.46), channel_id=1, source_target_pairs={{0,80},{1,49},{16,96},{17,65},{32,112},{33,81},{48,0},{49,97},{64,... | collective-permute-start | bytes 393224 | tf_op jit(solution)/shard_map/ppermute | solution.py:37
  76.8 3.2 %collective-permute-start.17 = (bf16[128,512]{1,0:T(8,128)(2,1)}, bf16[128,512]{1,0:T(8,128)(2,1)S(1)}, u32[]{:S(2)}, u32[]{:S(2)}) collective-permute-start(bf16[128,512]{1,0:T(8,128)(2,1)} %get-tuple-element.47), channel_id=1, source_target_pairs={{0,48},{1,81},{16,64},{17,97},{32,80},{33,113},{48,96},{49,1},{64,... | collective-permute-start | bytes 393224 | tf_op jit(solution)/shard_map/ppermute | solution.py:37
  80.0 0.0 collective-permute-start.18
  80.0 3.6 %collective-permute-start.19 = (bf16[128,512]{1,0:T(8,128)(2,1)}, bf16[128,512]{1,0:T(8,128)(2,1)S(1)}, u32[]{:S(2)}, u32[]{:S(2)}) collective-permute-start(bf16[128,512]{1,0:T(8,128)(2,1)} %get-tuple-element.49), channel_id=1, source_target_pairs={{0,32},{1,97},{16,48},{17,113},{32,64},{33,1},{48,80},{49,17},{64,... | collective-permute-start | bytes 393224 | tf_op jit(solution)/shard_map/ppermute | solution.py:37
  83.6 0.6 collective-permute-done.15
  84.1 2.1 %collective-permute-start.20 = (bf16[128,512]{1,0:T(8,128)(2,1)}, bf16[128,512]{1,0:T(8,128)(2,1)S(1)}, u32[]{:S(2)}, u32[]{:S(2)}) collective-permute-start(bf16[128,512]{1,0:T(8,128)(2,1)} %get-tuple-element.50), channel_id=1, source_target_pairs={{0,112},{1,17},{16,0},{17,33},{32,16},{33,49},{48,32},{49,65},{64,... | collective-permute-start | bytes 393224 | tf_op jit(solution)/shard_map/ppermute | solution.py:37
  86.3 0.4 collective-permute-done.16
  86.7 3.3 %collective-permute-start.21 = (bf16[128,512]{1,0:T(8,128)(2,1)}, bf16[128,512]{1,0:T(8,128)(2,1)S(1)}, u32[]{:S(2)}, u32[]{:S(2)}) collective-permute-start(bf16[128,512]{1,0:T(8,128)(2,1)} %get-tuple-element.51), channel_id=1, source_target_pairs={{0,16},{1,113},{16,32},{17,1},{32,48},{33,17},{48,64},{49,33},{64,... | collective-permute-start | bytes 393224 | tf_op jit(solution)/shard_map/ppermute | solution.py:37
  90.0 7.3 %all-to-all-done.parts = bf16[16,256,256]{2,1,0:T(8,128)(2,1)S(1)} async-done(((bf16[16,256,256]{2,1,0:T(8,128)(2,1)}), bf16[16,256,256]{2,1,0:T(8,128)(2,1)S(1)}, u32[]{:S(2)}, u32[]{:S(2)}) %all-to-all-start) | async-done | bytes 2097184 | tf_op jit(solution)/shard_map/all_to_all | solution.py:386
  97.2 0.9 shard_map.57
  98.1 0.0 collective-permute-done.17
  98.1 1.3 %collective-permute-start.22 = (f32[2,128,128]{2,1,0:T(8,128)S(1)}, f32[2,128,128]{2,1,0:T(8,128)S(1)}, u32[]{:S(2)}, u32[]{:S(2)}) collective-permute-start(f32[2,128,128]{2,1,0:T(8,128)S(1)} %get-tuple-element.57), channel_id=1, source_target_pairs={{0,1},{1,0},{2,3},{3,2},{4,5},{5,4},{6,7},{7,6},{8,9},{9,8},{10,11... | collective-permute-start | bytes 393224 | tf_op jit(solution)/shard_map/ppermute | solution.py:41
  99.5 0.0 collective-permute-done.18
  99.5 0.0 collective-permute-done.19
  99.5 0.0 collective-permute-done.20
  99.5 0.7 collective-permute-done.21
  100.2 0.0 copy-done
  100.2 0.8 multiply_bitcast_fusion
  101.1 0.0 collective-permute-done.22.received
  101.1 1.3 %shard_map.58 = f32[4,128,128]{2,1,0:T(8,128)} custom-call(s32[4]{0:T(128)S(1)} %pad_add_fusion.position, f32[2,128,128]{2,1,0:T(8,128)S(1)} %get-tuple-element.56.keep, f32[2,128,128]{2,1,0:T(8,128)S(1)} %collective-permute-done.22.received), custom_call_target="tpu_custom_call" | custom-call | bytes 2097152 | tf_op jit(solution)/shard_map/pallas_call | solution.py:410
  (10 shorter events, 0.2 us)
Async XLA Ops:
  3.1 4.3 %collective-permute-start = (bf16[1,144,512]{2,1,0:T(8,128)(2,1)S(1)}, bf16[1,144,512]{2,1,0:T(8,128)(2,1)S(1)}, u32[]{:S(2)}, u32[]{:S(2)}) collective-permute-start(bf16[1,144,512]{2,1,0:T(8,128)(2,1)S(1)} %get-tuple-element.30), channel_id=1, source_target_pairs={{0,1},{1,0},{2,3},{3,2},{4,5},{5,4},{6,7},{7,6},{8,9},{9,8},{10,11... | collective-permute-start | bytes 442376 | tf_op jit(solution)/shard_map/ppermute | solution.py:41
  7.4 10.0 %collective-permute-start.2 = (bf16[2,144,512]{2,1,0:T(8,128)(2,1)S(1)}, bf16[2,144,512]{2,1,0:T(8,128)(2,1)S(1)}, u32[]{:S(2)}, u32[]{:S(2)}) collective-permute-start(bf16[2,144,512]{2,1,0:T(8,128)(2,1)S(1)} %constant_dynamic-update-slice_fusion.chip), channel_id=1, source_target_pairs={{0,32},{1,97},{16,48},{17,113},{32,64},{33,1},{48,80},{49,17},{64,... | collective-permute-start | bytes 884744 | tf_op jit(solution)/shard_map/ppermute | solution.py:37
  11.8 10.8 %collective-permute-start.1 = (bf16[2,144,512]{2,1,0:T(8,128)(2,1)S(1)}, bf16[2,144,512]{2,1,0:T(8,128)(2,1)S(1)}, u32[]{:S(2)}, u32[]{:S(2)}) collective-permute-start(bf16[2,144,512]{2,1,0:T(8,128)(2,1)S(1)} %constant_dynamic-update-slice_fusion.chip), channel_id=1, source_target_pairs={{0,16},{1,113},{16,32},{17,1},{32,48},{33,17},{48,64},{49,33},{64,... | collective-permute-start | bytes 884744 | tf_op jit(solution)/shard_map/ppermute | solution.py:37
  12.5 10.6 %collective-permute-start.4 = (bf16[4,128,512]{2,1,0:T(8,128)(2,1)S(1)}, bf16[4,128,512]{2,1,0:T(8,128)(2,1)S(1)}, u32[]{:S(2)}, u32[]{:S(2)}) collective-permute-start(bf16[4,128,512]{2,1,0:T(8,128)(2,1)S(1)} %get-tuple-element.31.v0), channel_id=1, source_target_pairs={{0,4},{1,13},{4,8},{5,1},{8,12},{9,5},{12,0},{13,9},{2,6},{3,15},{... | collective-permute-start | bytes 1572872 | tf_op jit(solution)/shard_map/ppermute | solution.py:37
  17.4 9.0 %collective-permute-start.7 = (bf16[2,144,512]{2,1,0:T(8,128)(2,1)S(1)}, bf16[2,144,512]{2,1,0:T(8,128)(2,1)S(1)}, u32[]{:S(2)}, u32[]{:S(2)}) collective-permute-start(bf16[2,144,512]{2,1,0:T(8,128)(2,1)S(1)} %collective-permute-done.2), channel_id=1, source_target_pairs={{0,16},{1,113},{16,32},{17,1},{32,48},{33,17},{48,64},{49,33},{64,... | collective-permute-start | bytes 884744 | tf_op jit(solution)/shard_map/ppermute | solution.py:37
  21.9 6.8 %collective-permute-start.8 = (bf16[1,144,512]{2,1,0:T(8,128)(2,1)S(1)}, bf16[1,144,512]{2,1,0:T(8,128)(2,1)S(1)}, u32[]{:S(2)}, u32[]{:S(2)}) collective-permute-start(bf16[1,144,512]{2,1,0:T(8,128)(2,1)S(1)} %slice.22), channel_id=1, source_target_pairs={{0,32},{1,97},{16,48},{17,113},{32,64},{33,1},{48,80},{49,17},{64,... | collective-permute-start | bytes 442376 | tf_op jit(solution)/shard_map/ppermute | solution.py:37
  22.7 17.0 %collective-permute-start.3 = (bf16[4,144,512]{2,1,0:T(8,128)(2,1)S(1)}, bf16[4,144,512]{2,1,0:T(8,128)(2,1)S(1)}, u32[]{:S(2)}, u32[]{:S(2)}) collective-permute-start(bf16[4,144,512]{2,1,0:T(8,128)(2,1)S(1)} %constant_dynamic-update-slice_fusion.2.near), channel_id=1, source_target_pairs={{0,1},{1,0},{2,3},{3,2},{4,5},{5,4},{6,7},{7,6},{8,9},{9,8},{10,11... | collective-permute-start | bytes 1769480 | tf_op jit(solution)/shard_map/ppermute | solution.py:41
  23.2 19.5 %collective-permute-start.11 = (bf16[4,128,512]{2,1,0:T(8,128)(2,1)S(1)}, bf16[4,128,512]{2,1,0:T(8,128)(2,1)S(1)}, u32[]{:S(2)}, u32[]{:S(2)}) collective-permute-start(bf16[4,128,512]{2,1,0:T(8,128)(2,1)S(1)} %collective-permute-done.4.v1), channel_id=1, source_target_pairs={{0,128},{1,131},{128,2},{129,1},{2,130},{3,129},{130,0},{131,3},{4... | collective-permute-start | bytes 1572872 | tf_op jit(solution)/shard_map/ppermute | solution.py:37
  28.8 15.2 %collective-permute-start.9 = (bf16[3,144,512]{2,1,0:T(8,128)(2,1)S(1)}, bf16[3,144,512]{2,1,0:T(8,128)(2,1)S(1)}, u32[]{:S(2)}, u32[]{:S(2)}) collective-permute-start(bf16[3,144,512]{2,1,0:T(8,128)(2,1)S(1)} %constant_dynamic-update-slice_fusion.4.rest), channel_id=1, source_target_pairs={{0,1},{1,0},{2,3},{3,2},{4,5},{5,4},{6,7},{7,6},{8,9},{9,8},{10,11... | collective-permute-start | bytes 1327112 | tf_op jit(solution)/shard_map/ppermute | solution.py:41
  31.0 2.9 %collective-permute-start.6 = (bf16[2,128,512]{2,1,0:T(8,128)(2,1)S(1)}, bf16[2,128,512]{2,1,0:T(8,128)(2,1)S(1)}, u32[]{:S(2)}, u32[]{:S(2)}) collective-permute-start(bf16[2,128,512]{2,1,0:T(8,128)(2,1)S(1)} %get-tuple-element.58), channel_id=1, source_target_pairs={{0,1},{1,0},{2,3},{3,2},{4,5},{5,4},{6,7},{7,6},{8,9},{9,8},{10,11... | collective-permute-start | bytes 786440 | tf_op jit(solution)/shard_map/ppermute | solution.py:41
  31.1 6.1 %collective-permute-start.5 = (bf16[2,128,512]{2,1,0:T(8,128)(2,1)S(1)}, bf16[2,128,512]{2,1,0:T(8,128)(2,1)S(1)}, u32[]{:S(2)}, u32[]{:S(2)}) collective-permute-start(bf16[2,128,512]{2,1,0:T(8,128)(2,1)S(1)} %get-tuple-element.59), channel_id=1, source_target_pairs={{0,4},{1,13},{4,8},{5,1},{8,12},{9,5},{12,0},{13,9},{2,6},{3,15},{... | collective-permute-start | bytes 786440 | tf_op jit(solution)/shard_map/ppermute | solution.py:37
  33.9 13.3 %collective-permute-start.10 = (bf16[2,128,512]{2,1,0:T(8,128)(2,1)S(1)}, bf16[2,128,512]{2,1,0:T(8,128)(2,1)S(1)}, u32[]{:S(2)}, u32[]{:S(2)}) collective-permute-start(bf16[2,128,512]{2,1,0:T(8,128)(2,1)S(1)} %slice.18), channel_id=1, source_target_pairs={{0,128},{1,131},{128,2},{129,1},{2,130},{3,129},{130,0},{131,3},{4... | collective-permute-start | bytes 786440 | tf_op jit(solution)/shard_map/ppermute | solution.py:37
  37.2 10.0 %collective-permute-start.12 = (bf16[2,128,512]{2,1,0:T(8,128)(2,1)S(1)}, bf16[2,128,512]{2,1,0:T(8,128)(2,1)S(1)}, u32[]{:S(2)}, u32[]{:S(2)}) collective-permute-start(bf16[2,128,512]{2,1,0:T(8,128)(2,1)S(1)} %collective-permute-done.5.v2), channel_id=1, source_target_pairs={{0,128},{1,131},{128,2},{129,1},{2,130},{3,129},{130,0},{131,3},{4... | collective-permute-start | bytes 786440 | tf_op jit(solution)/shard_map/ppermute | solution.py:37
  42.8 4.5 %collective-permute-start.13 = (bf16[2,128,512]{2,1,0:T(8,128)(2,1)S(1)}, bf16[2,128,512]{2,1,0:T(8,128)(2,1)S(1)}, u32[]{:S(2)}, u32[]{:S(2)}) collective-permute-start(bf16[2,128,512]{2,1,0:T(8,128)(2,1)S(1)} %slice.23), channel_id=1, source_target_pairs={{0,1},{1,0},{2,3},{3,2},{4,5},{5,4},{6,7},{7,6},{8,9},{9,8},{10,11... | collective-permute-start | bytes 786440 | tf_op jit(solution)/shard_map/ppermute | solution.py:41
  57.6 5.4 %copy-start.1 = (bf16[1024,512]{1,0:T(8,128)(2,1)S(1)}, bf16[1024,512]{1,0:T(8,128)(2,1)}, u32[]{:S(2)}) copy-start(bf16[1024,512]{1,0:T(8,128)(2,1)} %get-tuple-element.44) | copy-start | bytes 3145732
  57.6 39.6 %all-to-all-start = ((bf16[16,256,256]{2,1,0:T(8,128)(2,1)}), bf16[16,256,256]{2,1,0:T(8,128)(2,1)S(1)}, u32[]{:S(2)}, u32[]{:S(2)}) async-start(bf16[16,256,256]{2,1,0:T(8,128)(2,1)} %shard_map.56), calls=%async_computation | async-start | bytes 4194304 | tf_op jit(solution)/shard_map/all_to_all | solution.py:386
  63.1 2.7 %collective-permute-start.14 = (bf16[1024,512]{1,0:T(8,128)(2,1)S(1)}, bf16[1024,512]{1,0:T(8,128)(2,1)S(1)}, u32[]{:S(2)}, u32[]{:S(2)}) collective-permute-start(bf16[1024,512]{1,0:T(8,128)(2,1)S(1)} %copy-done.1), channel_id=1, source_target_pairs={{0,1},{1,0},{2,3},{3,2},{4,5},{5,4},{6,7},{7,6},{8,9},{9,8},{10,11... | collective-permute-start | bytes 3145736 | tf_op jit(solution)/shard_map/ppermute | solution.py:41
  71.6 28.6 %copy-start = (bf16[128,512]{1,0:T(8,128)(2,1)S(1)}, bf16[128,512]{1,0:T(8,128)(2,1)}, u32[]{:S(2)}) copy-start(bf16[128,512]{1,0:T(8,128)(2,1)} %get-tuple-element.52) | copy-start | bytes 393220
  71.6 12.5 %collective-permute-start.15 = (bf16[128,512]{1,0:T(8,128)(2,1)}, bf16[128,512]{1,0:T(8,128)(2,1)S(1)}, u32[]{:S(2)}, u32[]{:S(2)}) collective-permute-start(bf16[128,512]{1,0:T(8,128)(2,1)} %get-tuple-element.45), channel_id=1, source_target_pairs={{0,64},{1,65},{16,80},{17,81},{32,96},{33,97},{48,112},{49,113},{6... | collective-permute-start | bytes 393224 | tf_op jit(solution)/shard_map/ppermute | solution.py:37
  75.5 11.2 %collective-permute-start.16 = (bf16[128,512]{1,0:T(8,128)(2,1)}, bf16[128,512]{1,0:T(8,128)(2,1)S(1)}, u32[]{:S(2)}, u32[]{:S(2)}) collective-permute-start(bf16[128,512]{1,0:T(8,128)(2,1)} %get-tuple-element.46), channel_id=1, source_target_pairs={{0,80},{1,49},{16,96},{17,65},{32,112},{33,81},{48,0},{49,97},{64,... | collective-permute-start | bytes 393224 | tf_op jit(solution)/shard_map/ppermute | solution.py:37
  76.8 21.3 %collective-permute-start.17 = (bf16[128,512]{1,0:T(8,128)(2,1)}, bf16[128,512]{1,0:T(8,128)(2,1)S(1)}, u32[]{:S(2)}, u32[]{:S(2)}) collective-permute-start(bf16[128,512]{1,0:T(8,128)(2,1)} %get-tuple-element.47), channel_id=1, source_target_pairs={{0,48},{1,81},{16,64},{17,97},{32,80},{33,113},{48,96},{49,1},{64,... | collective-permute-start | bytes 393224 | tf_op jit(solution)/shard_map/ppermute | solution.py:37
  80.0 19.5 %collective-permute-start.18 = (bf16[128,512]{1,0:T(8,128)(2,1)}, bf16[128,512]{1,0:T(8,128)(2,1)S(1)}, u32[]{:S(2)}, u32[]{:S(2)}) collective-permute-start(bf16[128,512]{1,0:T(8,128)(2,1)} %get-tuple-element.48), channel_id=1, source_target_pairs={{0,96},{1,33},{16,112},{17,49},{32,0},{33,65},{48,16},{49,81},{64,... | collective-permute-start | bytes 393224 | tf_op jit(solution)/shard_map/ppermute | solution.py:37
  80.0 19.5 %collective-permute-start.19 = (bf16[128,512]{1,0:T(8,128)(2,1)}, bf16[128,512]{1,0:T(8,128)(2,1)S(1)}, u32[]{:S(2)}, u32[]{:S(2)}) collective-permute-start(bf16[128,512]{1,0:T(8,128)(2,1)} %get-tuple-element.49), channel_id=1, source_target_pairs={{0,32},{1,97},{16,48},{17,113},{32,64},{33,1},{48,80},{49,17},{64,... | collective-permute-start | bytes 393224 | tf_op jit(solution)/shard_map/ppermute | solution.py:37
  84.1 15.3 %collective-permute-start.20 = (bf16[128,512]{1,0:T(8,128)(2,1)}, bf16[128,512]{1,0:T(8,128)(2,1)S(1)}, u32[]{:S(2)}, u32[]{:S(2)}) collective-permute-start(bf16[128,512]{1,0:T(8,128)(2,1)} %get-tuple-element.50), channel_id=1, source_target_pairs={{0,112},{1,17},{16,0},{17,33},{32,16},{33,49},{48,32},{49,65},{64,... | collective-permute-start | bytes 393224 | tf_op jit(solution)/shard_map/ppermute | solution.py:37
  86.7 13.6 %collective-permute-start.21 = (bf16[128,512]{1,0:T(8,128)(2,1)}, bf16[128,512]{1,0:T(8,128)(2,1)S(1)}, u32[]{:S(2)}, u32[]{:S(2)}) collective-permute-start(bf16[128,512]{1,0:T(8,128)(2,1)} %get-tuple-element.51), channel_id=1, source_target_pairs={{0,16},{1,113},{16,32},{17,1},{32,48},{33,17},{48,64},{49,33},{64,... | collective-permute-start | bytes 393224 | tf_op jit(solution)/shard_map/ppermute | solution.py:37
  98.1 2.9 %collective-permute-start.22 = (f32[2,128,128]{2,1,0:T(8,128)S(1)}, f32[2,128,128]{2,1,0:T(8,128)S(1)}, u32[]{:S(2)}, u32[]{:S(2)}) collective-permute-start(f32[2,128,128]{2,1,0:T(8,128)S(1)} %get-tuple-element.57), channel_id=1, source_target_pairs={{0,1},{1,0},{2,3},{3,2},{4,5},{5,4},{6,7},{7,6},{8,9},{9,8},{10,11... | collective-permute-start | bytes 393224 | tf_op jit(solution)/shard_map/ppermute | solution.py:41
